TPU v7x, 128 devices: a whole 4x4x4 slice. The times are simulated.
128 devices in a mesh: shot: 8 (over y_lo, z), gx: 4 (over x), gy: 4 (over y_hi, core).
Axes of the slice: x: 4, y: 4 (y_hi: 2, y_lo: 2; y = y_hi * 2 + y_lo), z: 4, core: 2. Of those that a mesh axis runs over, the one named last changes fastest.
Arguments:
- stiffness: float32 [192, 64, 256], P('gx', 'gy'), may hold values from 0.03 to 0.1
- buoyancy: float32 [192, 64, 256], P('gx', 'gy'), may hold values from 0.05 to 1.6
- fwd_prev: float32 [8, 192, 64, 256], P('shot', 'gx', 'gy'), may hold values from -6 to 6
- fwd_now: float32 [8, 192, 64, 256], P('shot', 'gx', 'gy'), may hold values from -6 to 6
- adj_prev: float32 [8, 192, 64, 256], P('shot', 'gx', 'gy'), may hold values from -6 to 6
- adj_now: float32 [8, 192, 64, 256], P('shot', 'gx', 'gy'), may hold values from -6 to 6
- wavelet: float32 [8, 4], P('shot'), may hold values from -160 to 160
- source_cell: int32 [8, 3], P('shot'), may hold values from 0 to 255, as said below
- receiver_cell: int32 [8, 512, 3], P('shot'), may hold values from 0 to 255, as said below
- traces: float32 [8, 512, 4], P('shot'), may hold values from -60 to 60
- aperture_blocks: int32 [8, 4, 4, 8, 1], replicated, may hold values from 0 to 2, as said below
- aperture_count: int32 [8, 4, 4, 8], replicated, may hold values from 0 to 1, as said below
Outputs:
- fwd_final: float32 [8, 192, 64, 256], P('shot', 'gx', 'gy')
- adj_final: float32 [8, 192, 64, 256], P('shot', 'gx', 'gy')
- gradient: float32 [4, 24, 32, 128], P('gx', 'shot', 'gy')
Inputs may be any that keep to these rules, and one draw needn't show every extreme that they name: `aperture_blocks`: entries of one list are distinct local coarse rows, 0 to 2. `aperture_count`: some list is full and some empty in every draw; slots past the count hold rows that are to be ignored. `source_cell`: each entry is a cell inside the grid: x below 192, y below 64, depth below 256. `receiver_cell`: each entry is a cell inside the grid: x below 192, y below 64, depth below 256; cells may repeat.
All inputs are finite; a program needn't handle non-finite values.
Results may differ from a plain program's by a relative error of at most 0.024.
Values sent between devices are 32-bit elements; how exact they have to be, the bound alone decides.
A program may use at most 128 MiB of HBM per device.

v0:
```python
import jax
import jax.numpy as jnp
from jax import lax
from jax.sharding import PartitionSpec as P

second_coef = (-205.0 / 72.0, 8.0 / 5.0, -1.0 / 5.0, 8.0 / 315.0, -1.0 / 560.0)
first_coef = (4.0 / 5.0, -1.0 / 5.0, 4.0 / 105.0, -1.0 / 280.0)


def with_halo(cells, sides, width):
    for axis, dim in sides:
        count = lax.axis_size(axis)
        ends = count - 1
        head = lax.slice_in_dim(cells, 0, width, axis=dim)
        tail = lax.slice_in_dim(cells, cells.shape[dim] - width, cells.shape[dim], axis=dim)
        cells = jnp.concatenate(
            [
                lax.ppermute(tail, axis, [(i, (i + 1) % count) for i in range(ends)]),
                cells,
                lax.ppermute(head, axis, [((i + 1) % count, i) for i in range(ends)]),
            ],
            axis=dim,
        )
    return cells


def shifted(extended, along, offset, sizes):
    starts = [4, 4, 4]
    starts[along] = 4 + offset
    return extended[
        starts[0] : starts[0] + sizes[0],
        starts[1] : starts[1] + sizes[1],
        starts[2] : starts[2] + sizes[2],
    ]


def derivatives(padded):
    sizes = (padded.shape[0] - 8, padded.shape[1] - 8, padded.shape[2])
    extended = jnp.pad(padded, ((0, 0), (0, 0), (4, 4)))
    center = shifted(extended, 0, 0, sizes)
    laplace = 3.0 * second_coef[0] * center
    firsts = []
    for along in range(3):
        slope = jnp.zeros(sizes, jnp.float32)
        for reach in range(1, 5):
            ahead = shifted(extended, along, reach, sizes)
            behind = shifted(extended, along, -reach, sizes)
            laplace = laplace + second_coef[reach] * (ahead + behind)
            slope = slope + first_coef[reach - 1] * (ahead - behind)
        firsts.append(slope)
    return (laplace, firsts)


def operator_apply(padded, buoyancy, slopes):
    laplace, firsts = derivatives(padded)
    return (
        buoyancy * laplace + slopes[0] * firsts[0] + slopes[1] * firsts[1] + slopes[2] * firsts[2]
    )


def body(
    stiffness,
    buoyancy,
    fwd_prev,
    fwd_now,
    adj_prev,
    adj_now,
    wavelet,
    source_cell,
    receiver_cell,
    traces,
    aperture_blocks,
    aperture_count,
):
    rows_x, rows_y, depth = stiffness.shape
    tile_x = lax.axis_index("gx")
    tile_y = lax.axis_index("gy")
    shot_me = lax.axis_index("shot")
    base_x = tile_x * rows_x
    base_y = tile_y * rows_y
    steps_total = wavelet.shape[1]
    forward = [fwd_prev[0], fwd_now[0]]
    adjoint = [adj_prev[0], adj_now[0]]
    model_padded = with_halo(buoyancy, (("gx", 0), ("gy", 1)), 4)
    unused, slopes = derivatives(model_padded)
    for step_index in range(steps_total):
        stacked = jnp.stack([forward[-1], adjoint[-1]])
        padded = with_halo(stacked, (("gx", 1), ("gy", 2)), 4)
        ext_x = rows_x + 2 * 0
        ext_y = rows_y + 2 * 0
        local_x = source_cell[0, 0] - base_x + 0
        local_y = source_cell[0, 1] - base_y + 0
        inside = (local_x >= 0) & (local_x < ext_x) & (local_y >= 0) & (local_y < ext_y)
        source_field = (
            jnp.zeros((ext_x, ext_y, depth), jnp.float32)
            .at[jnp.clip(local_x, 0, ext_x - 1), jnp.clip(local_y, 0, ext_y - 1), source_cell[0, 2]]
            .add(jnp.where(inside, wavelet[0, step_index], 0.0))
        )
        rec_x = receiver_cell[0, :, 0] - base_x + 0
        rec_y = receiver_cell[0, :, 1] - base_y + 0
        rec_inside = (rec_x >= 0) & (rec_x < ext_x) & (rec_y >= 0) & (rec_y < ext_y)
        values = jnp.where(rec_inside, traces[0, :, step_index], 0.0)
        record_field = (
            jnp.zeros((ext_x, ext_y, depth), jnp.float32)
            .at[
                jnp.clip(rec_x, 0, ext_x - 1), jnp.clip(rec_y, 0, ext_y - 1), receiver_cell[0, :, 2]
            ]
            .add(values)
        )
        source_field, record_field = (source_field, record_field)
        forward.append(
            2.0 * forward[-1]
            - forward[-2]
            + stiffness * operator_apply(padded[0], buoyancy, slopes)
            + source_field
        )
        adjoint.append(
            2.0 * adjoint[-1]
            - adjoint[-2]
            + stiffness * operator_apply(padded[1], buoyancy, slopes)
            + record_field
        )
    image = jnp.zeros((rows_x, rows_y, depth), jnp.float32)
    for later in range(2, steps_total + 2):
        image = image + adjoint[later] * (
            forward[steps_total + 3 - later]
            - 2.0 * forward[steps_total + 2 - later]
            + forward[steps_total + 1 - later]
        )
    coarse_x = rows_x // 2
    coarse_y = rows_y // 2
    coarse_z = depth // 2
    coarse = image.reshape(coarse_x, 2, coarse_y, 2, coarse_z, 2).mean(axis=(1, 3, 5))
    owners = lax.axis_size("shot")
    rows_own = coarse_x // owners
    slots = aperture_blocks.shape[4]
    mine_ids = aperture_blocks[shot_me, tile_x, tile_y]
    mine_counts = aperture_count[shot_me, tile_x, tile_y]
    valid = jnp.arange(slots)[None, :] < mine_counts[:, None]
    coarse_rows = coarse.reshape(owners, rows_own, coarse_y * coarse_z)
    outgoing = jnp.take_along_axis(coarse_rows, mine_ids[:, :, None], axis=1)
    outgoing = outgoing * valid[:, :, None].astype(jnp.float32)
    incoming = lax.all_to_all(outgoing, "shot", split_axis=0, concat_axis=0, tiled=True)
    incoming_ids = aperture_blocks[:, tile_x, tile_y, shot_me].reshape(-1)
    selector = (incoming_ids[:, None] == jnp.arange(rows_own)[None, :]).astype(jnp.float32)
    summed = jnp.dot(
        selector.T,
        incoming.reshape(-1, coarse_y * coarse_z),
        precision=lax.Precision.HIGHEST,
        preferred_element_type=jnp.float32,
    )
    gradient = summed.reshape(rows_own, coarse_y, coarse_z)
    return (forward[-1][None], adjoint[-1][None], gradient[None])


def solution(mesh):
    in_specs = (
        P("gx", "gy", None),
        P("gx", "gy", None),
        P("shot", "gx", "gy", None),
        P("shot", "gx", "gy", None),
        P("shot", "gx", "gy", None),
        P("shot", "gx", "gy", None),
        P("shot", None),
        P("shot", None),
        P("shot", None, None),
        P("shot", None, None),
        P(),
        P(),
    )
    out_specs = (
        P("shot", "gx", "gy", None),
        P("shot", "gx", "gy", None),
        P("gx", "shot", "gy", None),
    )
    return jax.shard_map(body, mesh=mesh, in_specs=in_specs, out_specs=out_specs, check_vma=False)
```

profile of v0, /device:TPU:1, one launch (start us, length us, event | category | flops | bytes accessed | tf_op | source)
XLA Modules:
  0.0 486.1 jit_solution(2017810527200565117)
XLA Ops:
  1.7 3.9 collective-permute-start.5
  8.9 4.0 collective-permute-start
  19.4 1.4 constant_dynamic-update-slice_fusion.7
  23.2 3.4 collective-permute-start.6
  26.7 4.7 collective-permute-start.7
  32.5 2.4 collective-permute-start.2
  34.9 2.7 collective-permute-start.3
  39.6 2.3 select_maximum_fusion
  42.0 4.5 collective-permute-done.3
  46.5 1.6 pad_maximum_fusion
  49.5 12.4 %fusion.175 = (f32[48,16,256]{2,1,0:T(8,128)S(1)}, f32[48,16,256]{2,1,0:T(8,128)}, f32[48,16,256]{2,1,0:T(8,128)}, f32[48,16,256]{2,1,0:T(8,128)}) fusion(f32[48,16,256]{2,1,0:T(8,128)S(1)} %copy-done.5, f32[48,16,256]{2,1,0:T(8,128)S(1)} %copy-done, f32[56,24,256]{2,1,0:T(8,128)S(1)} %get-tuple-element.74, f32[1,48,16,256]{3,2,1,0:T(8,128)} %param.22, ...), kind=kLoop, calls=%fused_computation.291 | loop fusion | flops 23986176 | bytes 34996224 | tf_op jit(solution)/shard_map/add | solution.py:112
  64.4 5.4 %fusion.141 = f32[48,16,256]{2,1,0:T(8,128)S(1)} fusion(f32[48,16,256]{2,1,0:T(8,128)} %param.20, f32[48,16,256]{2,1,0:T(8,128)S(1)} %copy-done, f32[56,24,256]{2,1,0:T(8,128)S(1)} %get-tuple-element.75, f32[1,48,16,256]{3,2,1,0:T(8,128)} %param.24, f32[1,48,16,256]{3,2,1,0:T(8,128)} %param.25, f32[48,16,256]{2,1,0:T(8,128)} %get-tuple-element.67, ...), kind=kLoop, calls=%fused_computation.246 | loop fusion | flops 15925248 | bytes 21037056 | tf_op jit(solution)/shard_map/add | solution.py:118
  69.9 31.9 %scatter_fusion = f32[48,16,256]{2,1,0:T(8,128)S(1)} fusion(f32[48,16,256]{2,1,0:T(8,128)S(1)} %fusion.141, s32[512]{0:T(512)S(1)} %bitcast.125, f32[512]{0:T(512)S(1)} %bitcast.151), kind=kCustom, calls=%fused_computation.1 | custom fusion | flops 512 | bytes 12288 | tf_op jit(solution)/shard_map/scatter-add | solution.py:108
  101.8 4.1 collective-permute-start.8
  107.9 3.8 collective-permute-done.9
  112.6 3.1 collective-permute-start.10
  115.8 1.9 collective-permute-start.11
  119.0 2.5 collective-permute-done.10
  121.5 5.6 %collective-permute-done.11 = f32[2,56,4,256]{3,2,1,0:T(4,128)S(1)} collective-permute-done((f32[2,56,4,256]{3,2,1,0:T(4,128)S(1)}, f32[2,56,4,256]{3,2,1,0:T(4,128)S(1)}, u32[]{:S(2)}, u32[]{:S(2)}) %collective-permute-start.11) | collective-permute-done | bytes 458784 | tf_op jit(solution)/shard_map/ppermute | solution.py:20
  130.1 3.8 fusion.123
  137.4 5.4 %fusion.105 = f32[48,16,256]{2,1,0:T(8,128)S(1)} fusion(f32[48,16,256]{2,1,0:T(8,128)} %param.20, f32[48,16,256]{2,1,0:T(8,128)} %param.21, f32[56,24,256]{2,1,0:T(8,128)S(1)} %get-tuple-element.73, f32[1,48,16,256]{3,2,1,0:T(8,128)} %param.25, f32[48,16,256]{2,1,0:T(8,128)} %get-tuple-element.67, f32[48,16,256]{2,1,0:T(8,128)} %get-tuple-element.66, ...), kind=kLoop, calls=%fused_computation.208 | loop fusion | flops 15925248 | bytes 21037056 | tf_op jit(solution)/shard_map/add | solution.py:118
  142.8 31.9 %scatter_fusion.1 = f32[48,16,256]{2,1,0:T(8,128)S(1)} fusion(f32[48,16,256]{2,1,0:T(8,128)S(1)} %fusion.105, s32[512]{0:T(512)S(1)} %bitcast.126, f32[512]{0:T(512)S(1)} %bitcast.150), kind=kCustom, calls=%fused_computation.2 | custom fusion | flops 512 | bytes 12288 | tf_op jit(solution)/shard_map/scatter-add | solution.py:108
  174.7 2.9 collective-permute-start.12
  179.6 3.8 collective-permute-done.13
  184.4 3.1 collective-permute-start.14
  187.5 1.9 collective-permute-start.15
  190.7 2.5 collective-permute-done.14
  193.2 5.7 %collective-permute-done.15 = f32[2,56,4,256]{3,2,1,0:T(4,128)} collective-permute-done((f32[2,56,4,256]{3,2,1,0:T(4,128)S(1)}, f32[2,56,4,256]{3,2,1,0:T(4,128)}, u32[]{:S(2)}, u32[]{:S(2)}) %collective-permute-start.15) | collective-permute-done | bytes 458784 | tf_op jit(solution)/shard_map/ppermute | solution.py:20
  198.9 1.5 pad_maximum_fusion.2
  203.0 3.8 fusion.87
  210.1 6.1 %fusion.69 = f32[48,16,256]{2,1,0:T(8,128)} fusion(f32[48,16,256]{2,1,0:T(8,128)} %param.20, f32[48,16,256]{2,1,0:T(8,128)} %param.21, f32[56,24,256]{2,1,0:T(8,128)S(1)} %get-tuple-element.71, f32[48,16,256]{2,1,0:T(8,128)} %get-tuple-element.67, f32[48,16,256]{2,1,0:T(8,128)} %get-tuple-element.66, f32[48,16,256]{2,1,0:T(8,128)} %get-tuple-element.65, ...), kind=kLoop, calls=%fused_computation.170 | loop fusion | flops 15925248 | bytes 21037056 | tf_op jit(solution)/shard_map/add | solution.py:118
  216.2 70.8 %scatter_fusion.2 = f32[48,16,256]{2,1,0:T(8,128)} fusion(f32[48,16,256]{2,1,0:T(8,128)} %fusion.69, s32[512]{0:T(512)S(1)} %bitcast.127, f32[512]{0:T(512)S(1)} %bitcast.149), kind=kCustom, calls=%fused_computation.3 | custom fusion | flops 512 | bytes 12288 | tf_op jit(solution)/shard_map/scatter-add | solution.py:108
  286.9 1.6 pad_maximum_fusion.22
  288.6 1.7 collective-permute-start.16
  292.6 3.5 collective-permute-done.17
  297.1 2.9 collective-permute-start.18
  300.1 2.4 collective-permute-start.19
  304.4 1.4 collective-permute-done.18
  305.8 5.9 %collective-permute-done.19 = f32[2,56,4,256]{3,2,1,0:T(4,128)} collective-permute-done((f32[2,56,4,256]{3,2,1,0:T(4,128)}, f32[2,56,4,256]{3,2,1,0:T(4,128)}, u32[]{:S(2)}, u32[]{:S(2)}) %collective-permute-start.19) | collective-permute-done | bytes 458784 | tf_op jit(solution)/shard_map/ppermute | solution.py:20
  311.7 1.6 pad_maximum_fusion.3
  315.4 4.5 fusion.33
  319.9 3.7 fusion.51
  327.3 72.1 %scatter_fusion.3 = f32[48,16,256]{2,1,0:T(8,128)} fusion(f32[48,16,256]{2,1,0:T(8,128)} %fusion.33, s32[512]{0:T(512)S(1)} %bitcast.128, f32[512]{0:T(512)S(1)} %bitcast.152), kind=kCustom, calls=%fused_computation.4 | custom fusion | flops 512 | bytes 12288 | tf_op jit(solution)/shard_map/scatter-add | solution.py:108
  399.4 4.2 fusion.177
  403.6 52.4 %reshape.369 = f32[24,2,8,2,128,2]{5,4,3,2,1,0:T(8,128)} reshape(f32[48,16,256]{2,1,0:T(8,128)} %fusion.177) | data formatting | bytes 1572864 | tf_op jit(solution)/shard_map/reshape | solution.py:133
  456.0 17.8 %reduce_sum.9 = f32[24,8,128]{2,1,0:T(8,128)S(1)} reduce(f32[24,2,8,2,128,2]{5,4,3,2,1,0:T(8,128)} %reshape.369, f32[]{:T(128)} %constant.131.clone.1), dimensions={1,3,5}, to_apply=%region_5.6 | reduce | flops 172032 | bytes 884740 | tf_op jit(solution)/shard_map/reduce_sum | solution.py:133
  475.2 5.1 %all-to-all-start = ((f32[8,1,1024]{2,1,0:T(1,128)}), f32[8,1,1024]{2,1,0:T(1,128)S(1)}, u32[]{:S(2)}, u32[]{:S(2)}) async-start(f32[8,1,1024]{2,1,0:T(1,128)} %copy.25), calls=%async_computation | async-start | bytes 65536 | tf_op jit(solution)/shard_map/all_to_all | solution.py:143
  481.2 4.1 all-to-all-done
  (142 shorter events, 43.8 us)
Async XLA Ops:
  0.6 17.4 %copy-start.39 = (s32[3]{0:T(128)S(1)}, s32[3]{0:T(128)}, u32[]{:S(2)}) copy-start(s32[3]{0:T(128)} %constant.143.clone.1) | copy-start | bytes 40
  0.6 18.8 %copy-start = (f32[48,16,256]{2,1,0:T(8,128)S(1)}, f32[48,16,256]{2,1,0:T(8,128)}, u32[]{:S(2)}) copy-start(f32[48,16,256]{2,1,0:T(8,128)} %param.21) | copy-start | bytes 2359300
  0.7 7.5 %copy-start.31 = (f32[1,48,16,256]{3,2,1,0:T(8,128)S(1)}, f32[1,48,16,256]{3,2,1,0:T(8,128)}, u32[]{:S(2)}) copy-start(f32[1,48,16,256]{3,2,1,0:T(8,128)} %param.25) | copy-start | bytes 2359300
  0.7 13.5 %copy-start.38 = (s32[1,3]{1,0:T(1,128)S(1)}, s32[1,3]{1,0:T(1,128)}, u32[]{:S(2)}) copy-start(s32[1,3]{1,0:T(1,128)} %param.27) | copy-start | bytes 40
  0.7 16.6 %copy-start.35 = (s32[1,512,3]{1,0,2:T(1,128)S(1)}, s32[1,512,3]{1,0,2:T(1,128)}, u32[]{:S(2)}) copy-start(s32[1,512,3]{1,0,2:T(1,128)} %param.28) | copy-start | bytes 18436
  0.7 16.7 %copy-start.36 = (f32[1,512,4]{1,2,0:T(4,128)S(1)}, f32[1,512,4]{1,2,0:T(4,128)}, u32[]{:S(2)}) copy-start(f32[1,512,4]{1,2,0:T(4,128)} %param.29) | copy-start | bytes 24580
  1.7 17.1 %collective-permute-start.5 = (f32[4,16,256]{2,1,0:T(8,128)S(1)}, f32[4,16,256]{2,1,0:T(8,128)S(1)}, u32[]{:S(2)}, u32[]{:S(2)}) collective-permute-start(f32[4,16,256]{2,1,0:T(8,128)S(1)} %get-tuple-element.98), channel_id=1, source_target_pairs={{0,4},{4,8},{8,12},{1,5},{5,9},{9,13},{2,6},{6,10},{10,14},{3,7},{... | collective-permute-start | bytes 196616 | tf_op jit(solution)/shard_map/ppermute | solution.py:18
  5.6 15.2 %collective-permute-start.4 = (f32[4,16,256]{2,1,0:T(8,128)S(1)}, f32[4,16,256]{2,1,0:T(8,128)S(1)}, u32[]{:S(2)}, u32[]{:S(2)}) collective-permute-start(f32[4,16,256]{2,1,0:T(8,128)S(1)} %get-tuple-element.97), channel_id=1, source_target_pairs={{4,0},{8,4},{12,8},{5,1},{9,5},{13,9},{6,2},{10,6},{14,10},{7,3},{... | collective-permute-start | bytes 196616 | tf_op jit(solution)/shard_map/ppermute | solution.py:20
  8.9 22.5 %collective-permute-start = (f32[2,4,16,256]{3,2,1,0:T(8,128)}, f32[2,4,16,256]{3,2,1,0:T(8,128)S(1)}, u32[]{:S(2)}, u32[]{:S(2)}) collective-permute-start(f32[2,4,16,256]{3,2,1,0:T(8,128)} %get-tuple-element.90), channel_id=1, source_target_pairs={{0,4},{4,8},{8,12},{1,5},{5,9},{9,13},{2,6},{6,10},{10,14},{3,7},{... | collective-permute-start | bytes 393224 | tf_op jit(solution)/shard_map/ppermute | solution.py:18
  12.9 18.5 %collective-permute-start.1 = (f32[2,4,16,256]{3,2,1,0:T(8,128)S(1)}, f32[2,4,16,256]{3,2,1,0:T(8,128)S(1)}, u32[]{:S(2)}, u32[]{:S(2)}) collective-permute-start(f32[2,4,16,256]{3,2,1,0:T(8,128)S(1)} %get-tuple-element.91), channel_id=1, source_target_pairs={{4,0},{8,4},{12,8},{5,1},{9,5},{13,9},{6,2},{10,6},{14,10},{7,3},{... | collective-permute-start | bytes 393224 | tf_op jit(solution)/shard_map/ppermute | solution.py:20
  20.9 16.7 %copy-start.37 = (f32[1,4]{1,0:T(1,128)S(1)}, f32[1,4]{1,0:T(1,128)}, u32[]{:S(2)}) copy-start(f32[1,4]{1,0:T(1,128)} %param.26) | copy-start | bytes 52
  23.2 16.4 %collective-permute-start.6 = (f32[56,4,256]{2,1,0:T(4,128)}, f32[56,4,256]{2,1,0:T(4,128)S(1)}, u32[]{:S(2)}, u32[]{:S(2)}) collective-permute-start(f32[56,4,256]{2,1,0:T(4,128)} %get-tuple-element.92), channel_id=1, source_target_pairs={{1,0},{2,1},{3,2},{5,4},{6,5},{7,6},{9,8},{10,9},{11,10},{13,12},{... | collective-permute-start | bytes 688136 | tf_op jit(solution)/shard_map/ppermute | solution.py:20
  26.7 13.0 %collective-permute-start.7 = (f32[56,4,256]{2,1,0:T(4,128)S(1)}, f32[56,4,256]{2,1,0:T(4,128)S(1)}, u32[]{:S(2)}, u32[]{:S(2)}) collective-permute-start(f32[56,4,256]{2,1,0:T(4,128)S(1)} %get-tuple-element.93), channel_id=1, source_target_pairs={{0,1},{1,2},{2,3},{4,5},{5,6},{6,7},{8,9},{9,10},{10,11},{12,13},{... | collective-permute-start | bytes 688136 | tf_op jit(solution)/shard_map/ppermute | solution.py:18
  32.5 9.5 %collective-permute-start.2 = (f32[2,56,4,256]{3,2,1,0:T(4,128)}, f32[2,56,4,256]{3,2,1,0:T(4,128)}, u32[]{:S(2)}, u32[]{:S(2)}) collective-permute-start(f32[2,56,4,256]{3,2,1,0:T(4,128)} %get-tuple-element.82), channel_id=1, source_target_pairs={{0,1},{1,2},{2,3},{4,5},{5,6},{6,7},{8,9},{9,10},{10,11},{12,13},{... | collective-permute-start | bytes 1376264 | tf_op jit(solution)/shard_map/ppermute | solution.py:18
  34.9 11.6 %collective-permute-start.3 = (f32[2,56,4,256]{3,2,1,0:T(4,128)}, f32[2,56,4,256]{3,2,1,0:T(4,128)}, u32[]{:S(2)}, u32[]{:S(2)}) collective-permute-start(f32[2,56,4,256]{3,2,1,0:T(4,128)} %get-tuple-element.83), channel_id=1, source_target_pairs={{1,0},{2,1},{3,2},{5,4},{6,5},{7,6},{9,8},{10,9},{11,10},{13,12},{... | collective-permute-start | bytes 1376264 | tf_op jit(solution)/shard_map/ppermute | solution.py:20
  39.6 8.5 %copy-start.34 = (f32[56,4,256]{2,1,0:T(4,128)}, f32[56,4,256]{2,1,0:T(4,128)S(1)}, u32[]{:S(2)}) copy-start(f32[56,4,256]{2,1,0:T(4,128)S(1)} %collective-permute-done.7) | copy-start | bytes 688132
  69.8 31.9 %copy-start.23 = (f32[48,16,256]{2,1,0:T(8,128)S(1)}, f32[48,16,256]{2,1,0:T(8,128)}, u32[]{:S(2)}) copy-start(f32[48,16,256]{2,1,0:T(8,128)} %copy-done.22) | copy-start | bytes 2359300
  101.8 6.1 %collective-permute-start.8 = (f32[2,4,16,256]{3,2,1,0:T(8,128)S(1)}, f32[2,4,16,256]{3,2,1,0:T(8,128)S(1)}, u32[]{:S(2)}, u32[]{:S(2)}) collective-permute-start(f32[2,4,16,256]{3,2,1,0:T(8,128)S(1)} %get-tuple-element.88), channel_id=1, source_target_pairs={{0,4},{4,8},{8,12},{1,5},{5,9},{9,13},{2,6},{6,10},{10,14},{3,7},{... | collective-permute-start | bytes 393224 | tf_op jit(solution)/shard_map/ppermute | solution.py:18
  105.9 5.7 %collective-permute-start.9 = (f32[2,4,16,256]{3,2,1,0:T(8,128)S(1)}, f32[2,4,16,256]{3,2,1,0:T(8,128)S(1)}, u32[]{:S(2)}, u32[]{:S(2)}) collective-permute-start(f32[2,4,16,256]{3,2,1,0:T(8,128)S(1)} %get-tuple-element.89), channel_id=1, source_target_pairs={{4,0},{8,4},{12,8},{5,1},{9,5},{13,9},{6,2},{10,6},{14,10},{7,3},{... | collective-permute-start | bytes 393224 | tf_op jit(solution)/shard_map/ppermute | solution.py:20
  112.6 8.9 %collective-permute-start.10 = (f32[2,56,4,256]{3,2,1,0:T(4,128)}, f32[2,56,4,256]{3,2,1,0:T(4,128)S(1)}, u32[]{:S(2)}, u32[]{:S(2)}) collective-permute-start(f32[2,56,4,256]{3,2,1,0:T(4,128)} %get-tuple-element.80), channel_id=1, source_target_pairs={{0,1},{1,2},{2,3},{4,5},{5,6},{6,7},{8,9},{9,10},{10,11},{12,13},{... | collective-permute-start | bytes 1376264 | tf_op jit(solution)/shard_map/ppermute | solution.py:18
  115.8 11.3 %collective-permute-start.11 = (f32[2,56,4,256]{3,2,1,0:T(4,128)S(1)}, f32[2,56,4,256]{3,2,1,0:T(4,128)S(1)}, u32[]{:S(2)}, u32[]{:S(2)}) collective-permute-start(f32[2,56,4,256]{3,2,1,0:T(4,128)S(1)} %get-tuple-element.81), channel_id=1, source_target_pairs={{1,0},{2,1},{3,2},{5,4},{6,5},{7,6},{9,8},{10,9},{11,10},{13,12},{... | collective-permute-start | bytes 1376264 | tf_op jit(solution)/shard_map/ppermute | solution.py:20
  127.5 1.6 copy-start.9
  127.5 1.8 copy-start.12
  127.5 2.0 copy-start.15
  127.6 2.3 copy-start.24
  127.6 2.5 copy-start.30
  142.8 31.9 %copy-start.19 = (f32[48,16,256]{2,1,0:T(8,128)S(1)}, f32[48,16,256]{2,1,0:T(8,128)}, u32[]{:S(2)}) copy-start(f32[48,16,256]{2,1,0:T(8,128)} %add.1226) | copy-start | bytes 2359300
  174.7 4.9 %collective-permute-start.12 = (f32[2,4,16,256]{3,2,1,0:T(8,128)S(1)}, f32[2,4,16,256]{3,2,1,0:T(8,128)S(1)}, u32[]{:S(2)}, u32[]{:S(2)}) collective-permute-start(f32[2,4,16,256]{3,2,1,0:T(8,128)S(1)} %get-tuple-element.86), channel_id=1, source_target_pairs={{0,4},{4,8},{8,12},{1,5},{5,9},{9,13},{2,6},{6,10},{10,14},{3,7},{... | collective-permute-start | bytes 393224 | tf_op jit(solution)/shard_map/ppermute | solution.py:18
  177.7 5.7 %collective-permute-start.13 = (f32[2,4,16,256]{3,2,1,0:T(8,128)S(1)}, f32[2,4,16,256]{3,2,1,0:T(8,128)S(1)}, u32[]{:S(2)}, u32[]{:S(2)}) collective-permute-start(f32[2,4,16,256]{3,2,1,0:T(8,128)S(1)} %get-tuple-element.87), channel_id=1, source_target_pairs={{4,0},{8,4},{12,8},{5,1},{9,5},{13,9},{6,2},{10,6},{14,10},{7,3},{... | collective-permute-start | bytes 393224 | tf_op jit(solution)/shard_map/ppermute | solution.py:20
  184.4 8.9 %collective-permute-start.14 = (f32[2,56,4,256]{3,2,1,0:T(4,128)}, f32[2,56,4,256]{3,2,1,0:T(4,128)S(1)}, u32[]{:S(2)}, u32[]{:S(2)}) collective-permute-start(f32[2,56,4,256]{3,2,1,0:T(4,128)} %get-tuple-element.78), channel_id=1, source_target_pairs={{0,1},{1,2},{2,3},{4,5},{5,6},{6,7},{8,9},{9,10},{10,11},{12,13},{... | collective-permute-start | bytes 1376264 | tf_op jit(solution)/shard_map/ppermute | solution.py:18
  187.5 11.4 %collective-permute-start.15 = (f32[2,56,4,256]{3,2,1,0:T(4,128)S(1)}, f32[2,56,4,256]{3,2,1,0:T(4,128)}, u32[]{:S(2)}, u32[]{:S(2)}) collective-permute-start(f32[2,56,4,256]{3,2,1,0:T(4,128)S(1)} %get-tuple-element.79), channel_id=1, source_target_pairs={{1,0},{2,1},{3,2},{5,4},{6,5},{7,6},{9,8},{10,9},{11,10},{13,12},{... | collective-permute-start | bytes 1376264 | tf_op jit(solution)/shard_map/ppermute | solution.py:20
  200.4 1.6 copy-start.10
  200.4 1.8 copy-start.13
  200.4 2.0 copy-start.16
  200.5 2.3 copy-start.20
  200.5 2.5 copy-start.25
  216.2 70.8 %copy-start.27 = (f32[48,16,256]{2,1,0:T(8,128)S(1)}, f32[48,16,256]{2,1,0:T(8,128)}, u32[]{:S(2)}) copy-start(f32[48,16,256]{2,1,0:T(8,128)} %add.1302) | copy-start | bytes 2359300
  286.9 9.1 %copy-start.4 = (f32[48,16,256]{2,1,0:T(8,128)S(1)}, f32[48,16,256]{2,1,0:T(8,128)}, u32[]{:S(2)}) copy-start(f32[48,16,256]{2,1,0:T(8,128)} %scatter_fusion.2) | copy-start | bytes 2359300
  288.6 4.0 collective-permute-start.16
  290.3 5.7 %collective-permute-start.17 = (f32[2,4,16,256]{3,2,1,0:T(8,128)S(1)}, f32[2,4,16,256]{3,2,1,0:T(8,128)S(1)}, u32[]{:S(2)}, u32[]{:S(2)}) collective-permute-start(f32[2,4,16,256]{3,2,1,0:T(8,128)S(1)} %get-tuple-element.85), channel_id=1, source_target_pairs={{4,0},{8,4},{12,8},{5,1},{9,5},{13,9},{6,2},{10,6},{14,10},{7,3},{... | collective-permute-start | bytes 393224 | tf_op jit(solution)/shard_map/ppermute | solution.py:20
  297.1 8.6 %collective-permute-start.18 = (f32[2,56,4,256]{3,2,1,0:T(4,128)}, f32[2,56,4,256]{3,2,1,0:T(4,128)}, u32[]{:S(2)}, u32[]{:S(2)}) collective-permute-start(f32[2,56,4,256]{3,2,1,0:T(4,128)} %get-tuple-element.76), channel_id=1, source_target_pairs={{0,1},{1,2},{2,3},{4,5},{5,6},{6,7},{8,9},{9,10},{10,11},{12,13},{... | collective-permute-start | bytes 1376264 | tf_op jit(solution)/shard_map/ppermute | solution.py:18
  300.1 11.6 %collective-permute-start.19 = (f32[2,56,4,256]{3,2,1,0:T(4,128)}, f32[2,56,4,256]{3,2,1,0:T(4,128)}, u32[]{:S(2)}, u32[]{:S(2)}) collective-permute-start(f32[2,56,4,256]{3,2,1,0:T(4,128)} %get-tuple-element.77), channel_id=1, source_target_pairs={{1,0},{2,1},{3,2},{5,4},{6,5},{7,6},{9,8},{10,9},{11,10},{13,12},{... | collective-permute-start | bytes 1376264 | tf_op jit(solution)/shard_map/ppermute | solution.py:20
  313.3 1.6 copy-start.11
  313.3 1.8 copy-start.14
  313.4 2.0 copy-start.17
  315.4 4.5 copy-start.21
  315.4 4.5 copy-start.28
  475.2 10.2 %all-to-all-start = ((f32[8,1,1024]{2,1,0:T(1,128)}), f32[8,1,1024]{2,1,0:T(1,128)S(1)}, u32[]{:S(2)}, u32[]{:S(2)}) async-start(f32[8,1,1024]{2,1,0:T(1,128)} %copy.25), calls=%async_computation | async-start | bytes 65536 | tf_op jit(solution)/shard_map/all_to_all | solution.py:143
  (13 other events, 14.5 us)
where the time goes:
time: 490 us; the launch traced here: 486 us
  other arithmetic  289 us (59%)
  local copies, waits for them, and re-layouts  82.7 us (17%)
  starting transfers between devices  56.9 us (12%)
  waiting for transfers between devices  44.8 us (9%)
  between operations  12.3 us (3%)
    scatter-add x4, other arithmetic, body(): record_field = jnp.zeros((ext_x, ext_y, depth), jnp.float32).at[jnp.clip(...  207 us
    reshape x1, local copies, waits for them, and re-layouts, body(): image.reshape(coarse_x, 2, coarse_y, 2, coarse_z, 2).mean(axis=(1, 3, 5))  52.4 us
    ppermute x10, starting transfers between devices, with_halo(): lax.ppermute(tail, axis, [(i, (i + 1) % count) for i in range(ends)])  33.1 us
    ppermute x10, waiting for transfers between devices, with_halo(): lax.ppermute(head, axis, [((i + 1) % count, i) for i in range(ends)])  32.8 us
    add x4, other arithmetic, body(): 2.0 * forward[-1] - forward[-2]  23.7 us
    add x4, other arithmetic, body(): 2.0 * adjoint[-1] - adjoint[-2]  21.4 us
    ppermute x10, starting transfers between devices, with_halo(): lax.ppermute(head, axis, [((i + 1) % count, i) for i in range(ends)])  18.8 us
    reduce_sum x1, other arithmetic, body(): image.reshape(coarse_x, 2, coarse_y, 2, coarse_z, 2).mean(axis=(1, 3, 5))  17.8 us
  transfers between devices with their start and end apart: 21, of which 14 were waited for; matrix products, arithmetic and copies ran while one was open for 3% of the time, Pallas kernels for 0%

commit v1 on v0

v1 whole, which is shorter than its diff:
```python
import jax
import jax.numpy as jnp
from jax import lax
from jax.experimental import pallas as pl
from jax.experimental.pallas import tpu as pltpu
from jax.sharding import PartitionSpec as P

MESH = pl.DeviceIdType.MESH
STEPS = 4
WIDTH = 4
CHUNK = 6
TOP = 8
LANES = 128

C1, D1 = 8.0 / 5.0, 4.0 / 5.0
second = tuple(c / C1 for c in (-205.0 / 72.0, 8.0 / 5.0, -1.0 / 5.0, 8.0 / 315.0, -1.0 / 560.0))
first = tuple(d / D1 for d in (4.0 / 5.0, -1.0 / 5.0, 4.0 / 105.0, -1.0 / 280.0))


def split(v):
    high = v.astype(jnp.bfloat16)
    return high, (v - high.astype(jnp.float32)).astype(jnp.bfloat16)


def dot(a, b):
    return jnp.dot(a, b, preferred_element_type=jnp.float32)


def dot_nt(a, b):
    return lax.dot_general(a, b, (((1,), (1,)), ((), ())), preferred_element_type=jnp.float32)


def kernel(
    stiff, buoy, fwd0, fwd1, adj0, adj1, wave, source, receiver, traces, blocks, counts,
    fwd_out, adj_out, grad_out,
    F, B, K, CO, R, Q, A, BH, BL, CZ, PZ, ZS, SM, TI, OUTG, INC,
    load_sem, bx_send, bx_recv, by_send, by_recv, x_send, x_recv, y_send, y_recv,
    out_sem, g_send, g_recv,
):
    nx, ny, nz = stiff.shape
    chunks = nx // CHUNK
    gx, gy, me = lax.axis_index("gx"), lax.axis_index("gy"), lax.axis_index("shot")
    last_x, last_y = lax.axis_size("gx") - 1, lax.axis_size("gy") - 1
    shots = lax.axis_size("shot")
    own = pl.ds(TOP, ny)
    sides_x = ((gx > 0, gx - 1), (gx < last_x, gx + 1))
    sides_y = ((gy > 0, gy - 1), (gy < last_y, gy + 1))

    loads = []
    for half in range(2):
        z = pl.ds(half * LANES, LANES)
        inner = pl.ds(WIDTH, nx)
        loads += [
            (buoy.at[:, :, z], B.at[inner, half, own, :]),
            (fwd1.at[0, :, :, z], F.at[1, 0, inner, half, own, :]),
            (adj1.at[0, :, :, z], F.at[1, 1, inner, half, own, :]),
            (stiff.at[:, :, z], K.at[:, half]),
            (fwd0.at[0, :, :, z], F.at[0, 0, inner, half, own, :]),
            (adj0.at[0, :, :, z], F.at[0, 1, inner, half, own, :]),
        ]
    loads = [pltpu.make_async_copy(s, d, load_sem.at[i]) for i, (s, d) in enumerate(loads)]
    for i in (0, 6, 1, 7, 2, 8, 3, 9, 4, 10, 5, 11):
        loads[i].start()

    barrier = pltpu.get_barrier_semaphore()
    peers = shots - 1
    for axis, sides in (("gx", sides_x), ("gy", sides_y)):
        for there, index in sides:
            @pl.when(there)
            def _():
                pl.semaphore_signal(barrier, inc=1, device_id={axis: index}, device_id_type=MESH)
            peers = peers + jnp.where(there, 1, 0)

    def greet(step, _):
        pl.semaphore_signal(
            barrier, inc=1, device_id={"shot": lax.rem(me + step, shots)}, device_id_type=MESH
        )
        return 0

    lax.fori_loop(1, shots, greet, 0)

    for side, (there, _) in enumerate(sides_x):
        @pl.when(jnp.logical_not(there))
        def _():
            at = pl.ds(side * (nx + WIDTH), WIDTH)
            B[at, :, own, :] = jnp.zeros((WIDTH, 2, ny, LANES), jnp.float32)
            for level in range(1, STEPS + 1):
                for field in range(2):
                    F[level, field, at, :, own, :] = jnp.zeros((WIDTH, 2, ny, LANES), jnp.float32)
    for side, (there, _) in enumerate(sides_y):
        @pl.when(jnp.logical_not(there))
        def _():
            at = pl.ds(TOP - WIDTH + side * (ny + WIDTH), WIDTH)

            def clear(x, _):
                B[x, :, at, :] = jnp.zeros((2, WIDTH, LANES), jnp.float32)
                for level in range(1, STEPS + 1):
                    for field in range(2):
                        F[level, field, x, :, at, :] = jnp.zeros((2, WIDTH, LANES), jnp.float32)
                return 0

            lax.fori_loop(WIDTH, nx + WIDTH, clear, 0)

    def x_edge(side):
        return pl.ds(WIDTH + side * (nx - WIDTH), WIDTH), pl.ds((1 - side) * (nx + WIDTH), WIDTH)

    def y_edge(side):
        return (
            pl.ds(TOP + side * (ny - WIDTH), WIDTH),
            pl.ds(TOP - WIDTH + (1 - side) * (ny + WIDTH), WIDTH),
        )

    def x_copy(level, side, index):
        mine, theirs = x_edge(side)
        return pltpu.make_async_remote_copy(
            src_ref=F.at[level, :, mine, :, own, :],
            dst_ref=F.at[level, :, theirs, :, own, :],
            send_sem=x_send.at[level, side],
            recv_sem=x_recv.at[level, 1 - side],
            device_id={"gx": index},
            device_id_type=MESH,
        )

    def x_arrival(level, side, index):
        _, here = x_edge(1 - side)
        return pltpu.make_async_remote_copy(
            src_ref=F.at[level, :, here, :, own, :],
            dst_ref=F.at[level, :, here, :, own, :],
            send_sem=x_send.at[level, side],
            recv_sem=x_recv.at[level, side],
            device_id={"gx": index},
            device_id_type=MESH,
        )

    def y_copy(level, chunk, side, index):
        mine, theirs = y_edge(side)
        x = pl.ds(WIDTH + chunk * CHUNK, CHUNK)
        return pltpu.make_async_remote_copy(
            src_ref=F.at[level, :, x, :, mine, :],
            dst_ref=F.at[level, :, x, :, theirs, :],
            send_sem=y_send.at[level, chunk, side],
            recv_sem=y_recv.at[level, chunk, 1 - side],
            device_id={"gy": index},
            device_id_type=MESH,
        )

    def y_arrival(level, chunk, side, index):
        _, here = y_edge(1 - side)
        x = pl.ds(WIDTH + chunk * CHUNK, CHUNK)
        return pltpu.make_async_remote_copy(
            src_ref=F.at[level, :, x, :, here, :],
            dst_ref=F.at[level, :, x, :, here, :],
            send_sem=y_send.at[level, chunk, side],
            recv_sem=y_recv.at[level, chunk, side],
            device_id={"gy": index},
            device_id_type=MESH,
        )

    def bx_copy(side, index, arrival=False):
        mine, theirs = x_edge(1 - side if arrival else side)
        return pltpu.make_async_remote_copy(
            src_ref=B.at[theirs if arrival else mine, :, own, :],
            dst_ref=B.at[theirs, :, own, :],
            send_sem=bx_send.at[side],
            recv_sem=bx_recv.at[side if arrival else 1 - side],
            device_id={"gx": index},
            device_id_type=MESH,
        )

    def by_copy(chunk, side, index, arrival=False):
        mine, theirs = y_edge(1 - side if arrival else side)
        x = pl.ds(WIDTH + chunk * CHUNK, CHUNK)
        return pltpu.make_async_remote_copy(
            src_ref=B.at[x, :, theirs if arrival else mine, :],
            dst_ref=B.at[x, :, theirs, :],
            send_sem=by_send.at[chunk, side],
            recv_sem=by_recv.at[chunk, side if arrival else 1 - side],
            device_id={"gy": index},
            device_id_type=MESH,
        )

    def for_sides(sides, do):
        for side, (there, index) in enumerate(sides):
            @pl.when(there)
            def _():
                do(side, index)

    def order(i):
        return lax.rem(chunks - i, chunks)

    for i in (0, 6, 1, 7, 2, 8):
        loads[i].wait()
    pl.semaphore_wait(barrier, peers)
    for_sides(sides_x, lambda side, index: bx_copy(side, index).start())
    for_sides(sides_x, lambda side, index: x_copy(1, side, index).start())

    def first_strips(i, _):
        chunk = order(i)

        def go(side, index):
            by_copy(chunk, side, index).start()
            y_copy(1, chunk, side, index).start()

        for_sides(sides_y, go)
        return 0

    lax.fori_loop(0, chunks, first_strips, 0)

    diff = lax.broadcasted_iota(jnp.int32, (nz, nz), 0) - lax.broadcasted_iota(jnp.int32, (nz, nz), 1)
    lap = jnp.zeros((nz, nz), jnp.float32)
    der = jnp.zeros((nz, nz), jnp.float32)
    for reach in range(1, WIDTH + 1):
        lap = jnp.where(jnp.abs(diff) == reach, second[reach], lap)
        der = jnp.where(diff == reach, first[reach - 1], der)
        der = jnp.where(diff == -reach, -first[reach - 1], der)
    CZ[:, 0:nz] = lap.astype(jnp.bfloat16)
    CZ[:, nz:] = der.astype(jnp.bfloat16)
    fine = lax.broadcasted_iota(jnp.int32, (nz, nz // 2), 0)
    pair = lax.broadcasted_iota(jnp.int32, (nz, nz // 2), 1) * 2
    PZ[...] = jnp.where((fine == pair) | (fine == pair + 1), 0.125, 0.0).astype(jnp.bfloat16)

    for half in range(2):
        row = lax.broadcasted_iota(jnp.int32, (ny, LANES), 0) + gy * ny
        col = lax.broadcasted_iota(jnp.int32, (ny, LANES), 1) + half * LANES
        SM[half] = jnp.where((row == source[0, 1]) & (col == source[0, 2]), 1.0, 0.0)

    rec_x = receiver[0] - gx * nx
    rec_y = receiver[1] - gy * ny
    inside = (rec_x >= 0) & (rec_x < nx) & (rec_y >= 0) & (rec_y < ny)
    cell = jnp.where(inside, rec_x * ny + rec_y, -1)
    nrec = cell.shape[1]
    rows = 128

    def hot(g, _):
        at = lax.broadcasted_iota(jnp.int32, (rows, nrec), 0) + g * rows
        A[pl.ds(pl.multiple_of(g * rows, rows), rows), :] = jnp.where(at == cell, 1.0, 0.0).astype(
            jnp.bfloat16
        )
        return 0

    lax.fori_loop(0, nx * ny // rows, hot, 0)
    rec_z = receiver[2]
    for n in range(STEPS):
        def place(g, _):
            at = lax.broadcasted_iota(jnp.int32, (64, nrec), 0) + g * 64
            high, low = split(jnp.where(at == rec_z, traces[0, n : n + 1, :], 0.0))
            where = pl.ds(pl.multiple_of(g * 64, 64), 64)
            BH[n, where, :] = high
            BL[n, where, :] = low
            return 0

        lax.fori_loop(0, nz // 64, place, 0)

    def inject(n, _):
        for part in range(2):
            hots = A[pl.ds(part * nx * ny // 2, nx * ny // 2), :]
            field = dot_nt(hots, BH[n]) + dot_nt(hots, BL[n])
            field = field.reshape(nx // 2, ny, nz)
            for half in range(2):
                R[n, pl.ds(part * nx // 2, nx // 2), half] = field[:, :, half * LANES : (half + 1) * LANES]
        return 0

    lax.fori_loop(0, STEPS, inject, 0)

    for i in (3, 9, 4, 10, 5, 11):
        loads[i].wait()

    def both_halves(ref, x):
        parts = [ref[x, half, own, :].reshape(CHUNK * ny, LANES) for half in range(2)]
        return jnp.concatenate(parts, axis=1)

    def slopes(ref, along, x, half):
        total = None
        for reach in range(1, WIDTH + 1):
            if along == 0:
                ahead, behind = ref[x + reach, half, own, :], ref[x - reach, half, own, :]
            else:
                ahead = ref[x, half, pl.ds(TOP + reach, ny), :]
                behind = ref[x, half, pl.ds(TOP - reach, ny), :]
            term = ahead - behind
            if reach > 1:
                term = first[reach - 1] * term
            total = term if total is None else total + term
        return total

    def coefficients(chunk):
        @pl.when(chunk == 0)
        def _():
            @pl.when(sides_x[0][0])
            def _():
                bx_copy(0, sides_x[0][1], True).wait_recv()

        @pl.when(chunk == chunks - 1)
        def _():
            @pl.when(sides_x[1][0])
            def _():
                bx_copy(1, sides_x[1][1], True).wait_recv()

        for_sides(sides_y, lambda side, index: by_copy(chunk, side, index, True).wait_recv())
        x0 = chunk * CHUNK
        high, low = split(both_halves(B, pl.ds(WIDTH + x0, CHUNK)))
        der_z = dot(high, CZ[:, nz:]) + dot(low, CZ[:, nz:])
        for half in range(2):
            ZS[0, 0, half] = der_z[:, half * LANES : (half + 1) * LANES]

        def plane(j, _):
            x = x0 + j
            for half in range(2):
                stiffness = K[x, half]
                CO[0, x, half] = C1 * stiffness * B[WIDTH + x, half, own, :]
                stiffness = (D1 * D1) * stiffness
                CO[1, x, half] = stiffness * slopes(B, 0, WIDTH + x, half)
                CO[2, x, half] = stiffness * slopes(B, 1, WIDTH + x, half)
                at = pl.ds(pl.multiple_of(j * ny, ny), ny)
                CO[3, x, half] = stiffness * ZS[0, 0, half, at, :]
            return 0

        lax.fori_loop(0, CHUNK, plane, 0)

    def advance(n, chunk):
        level = n + 1
        x0 = chunk * CHUNK

        @pl.when(chunk == 0)
        def _():
            @pl.when(sides_x[0][0])
            def _():
                x_arrival(level, 0, sides_x[0][1]).wait_recv()

        @pl.when(chunk == chunks - 1)
        def _():
            @pl.when(sides_x[1][0])
            def _():
                x_arrival(level, 1, sides_x[1][1]).wait_recv()

        for_sides(sides_y, lambda side, index: y_arrival(level, chunk, side, index).wait_recv())

        inner = pl.ds(WIDTH + x0, CHUNK)
        both = [both_halves(F.at[level, field], inner) for field in range(2)]
        high, low = split(jnp.concatenate(both, axis=0))
        along_z = dot(high, CZ[...]) + dot(low, CZ[...])
        for field in range(2):
            for kind in range(2):
                for half in range(2):
                    c0 = kind * nz + half * LANES
                    r0 = field * CHUNK * ny
                    ZS[field, kind, half] = along_z[r0 : r0 + CHUNK * ny, c0 : c0 + LANES]

        def plane(j, _):
            x = x0 + j
            xe = x + WIDTH
            at = pl.ds(pl.multiple_of(j * ny, ny), ny)
            amplitude = jnp.where(source[0, 0] - gx * nx == x, wave[0, n], 0.0)
            for half in range(2):
                co = [CO[i, x, half] for i in range(4)]
                for field in range(2):
                    ref = F.at[level, field]
                    now = ref[xe, half, own, :]
                    lap = (3.0 * second[0]) * now + ZS[field, 0, half, at, :]
                    der_x = der_y = None
                    for reach in range(1, WIDTH + 1):
                        xa, xb = ref[xe + reach, half, own, :], ref[xe - reach, half, own, :]
                        ya = ref[xe, half, pl.ds(TOP + reach, ny), :]
                        yb = ref[xe, half, pl.ds(TOP - reach, ny), :]
                        pairs = (xa + xb) + (ya + yb)
                        dx, dy = xa - xb, ya - yb
                        if reach == 1:
                            lap, der_x, der_y = lap + pairs, dx, dy
                        else:
                            lap = lap + second[reach] * pairs
                            der_x = der_x + first[reach - 1] * dx
                            der_y = der_y + first[reach - 1] * dy
                    change = co[0] * lap + co[1] * der_x + co[2] * der_y
                    change = change + co[3] * ZS[field, 1, half, at, :]
                    if field == 0:
                        change = change + amplitude * SM[half]
                        Q[n, x, half] = change
                    else:
                        change = change + R[n, x, half]
                    before = F[n, field, xe, half, own, :]
                    F[n + 2, field, xe, half, own, :] = (2.0 * now - before) + change
            return 0

        lax.fori_loop(0, CHUNK, plane, 0)

        @pl.when(n < STEPS - 1)
        def _():
            @pl.when(chunk == 0)
            def _():
                @pl.when(sides_x[0][0])
                def _():
                    x_copy(level + 1, 0, sides_x[0][1]).start()

            @pl.when(chunk == chunks - 1)
            def _():
                @pl.when(sides_x[1][0])
                def _():
                    x_copy(level + 1, 1, sides_x[1][1]).start()

            for_sides(sides_y, lambda side, index: y_copy(level + 1, chunk, side, index).start())

    def out_copies(chunk):
        x = pl.ds(chunk * CHUNK, CHUNK)
        xe = pl.ds(WIDTH + chunk * CHUNK, CHUNK)
        for field, out in enumerate((fwd_out, adj_out)):
            for half in range(2):
                yield pltpu.make_async_copy(
                    F.at[STEPS + 1, field, xe, half, own, :],
                    out.at[0, x, :, pl.ds(half * LANES, LANES)],
                    out_sem.at[chunk, field, half],
                )

    def grad_copy(owner, slot, sem):
        return pltpu.make_async_remote_copy(
            src_ref=OUTG.at[owner],
            dst_ref=INC.at[slot],
            send_sem=g_send.at[owner],
            recv_sem=g_recv.at[sem],
            device_id={"shot": owner},
            device_id_type=MESH,
        )

    def chosen(shot, owner, k):
        valid = (blocks[shot, gx, gy, 0, owner] == k) & (counts[shot, gx, gy, owner] > 0)
        return jnp.where(valid, 1.0, 0.0)

    def imaging(chunk):
        for copy in out_copies(chunk):
            copy.start()
        x0 = chunk * CHUNK
        for k in range(CHUNK // 2):
            for half in range(2):
                total = None
                for odd in range(2):
                    x = x0 + 2 * k + odd
                    for later in range(2, STEPS + 2):
                        term = F[later, 1, x + WIDTH, half, own, :] * Q[STEPS + 1 - later, x, half]
                        total = term if total is None else total + term
                TI[k, half] = total
        rows_k = []
        for k in range(CHUNK // 2):
            halves = [
                TI[k, half, pl.ds(0, ny // 2, stride=2), :] + TI[k, half, pl.ds(1, ny // 2, stride=2), :]
                for half in range(2)
            ]
            rows_k.append(jnp.concatenate(halves, axis=1))
        high, low = split(jnp.concatenate(rows_k, axis=0))
        coarse = dot(high, PZ[...]) + dot(low, PZ[...])
        row = None
        for k in range(CHUNK // 2):
            term = chosen(me, chunk, k) * coarse[k * (ny // 2) : (k + 1) * (ny // 2), :]
            row = term if row is None else row + term

        @pl.when(chunk == me)
        def _():
            INC[me] = row

        @pl.when(chunk != me)
        def _():
            OUTG[chunk] = row
            grad_copy(chunk, me, me).start()

    def run(t, _):
        n = t // chunks
        chunk = order(lax.rem(t, chunks))

        @pl.when(n == 0)
        def _():
            coefficients(chunk)

        advance(n, chunk)

        @pl.when(n == STEPS - 1)
        def _():
            imaging(chunk)

        return 0

    lax.fori_loop(0, STEPS * chunks, run, 0)

    def arrive(step, _):
        shot = lax.rem(me + step, shots)
        grad_copy(shot, shot, shot).wait_recv()
        return 0

    lax.fori_loop(1, shots, arrive, 0)
    for k in range(CHUNK // 2):
        total = None
        for shot in range(shots):
            term = chosen(shot, me, k) * INC[shot]
            total = term if total is None else total + term
        grad_out[0, k] = total

    def sent(step, _):
        grad_copy(lax.rem(me + step, shots), me, me).wait_send()
        return 0

    lax.fori_loop(1, shots, sent, 0)

    def done(chunk, _):
        for copy in out_copies(chunk):
            copy.wait()

        def strips(side, index):
            by_copy(chunk, side, index).wait_send()
            for level in range(1, STEPS + 1):
                y_copy(level, chunk, side, index).wait_send()

        for_sides(sides_y, strips)
        return 0

    lax.fori_loop(0, chunks, done, 0)

    def faces(side, index):
        bx_copy(side, index).wait_send()
        for level in range(1, STEPS + 1):
            x_copy(level, side, index).wait_send()

    for_sides(sides_x, faces)


def body(
    stiffness, buoyancy, fwd_prev, fwd_now, adj_prev, adj_now, wavelet, source_cell, receiver_cell,
    traces, aperture_blocks, aperture_count,
):
    nx, ny, nz = stiffness.shape
    shots = lax.axis_size("shot")
    nrec = traces.shape[1]
    chunks = nx // CHUNK
    xe, ye = nx + 2 * WIDTH, ny + 2 * TOP
    f32, bf16 = jnp.float32, jnp.bfloat16
    hbm = pl.BlockSpec(memory_space=pl.ANY)
    vmem = pl.BlockSpec(memory_space=pltpu.VMEM)
    smem = pl.BlockSpec(memory_space=pltpu.SMEM)
    dma = pltpu.SemaphoreType.DMA
    return pl.pallas_call(
        kernel,
        out_shape=(
            jax.ShapeDtypeStruct(fwd_now.shape, f32),
            jax.ShapeDtypeStruct(adj_now.shape, f32),
            jax.ShapeDtypeStruct((1, nx // 2 // shots, ny // 2, nz // 2), f32),
        ),
        in_specs=[hbm] * 6 + [smem] * 2 + [vmem] * 2 + [smem] * 2,
        out_specs=(hbm, hbm, vmem),
        scratch_shapes=[
            pltpu.VMEM((STEPS + 2, 2, xe, 2, ye, LANES), f32),
            pltpu.VMEM((xe, 2, ye, LANES), f32),
            pltpu.VMEM((nx, 2, ny, LANES), f32),
            pltpu.VMEM((4, nx, 2, ny, LANES), f32),
            pltpu.VMEM((STEPS, nx, 2, ny, LANES), f32),
            pltpu.VMEM((STEPS, nx, 2, ny, LANES), f32),
            pltpu.VMEM((nx * ny, nrec), bf16),
            pltpu.VMEM((STEPS, nz, nrec), bf16),
            pltpu.VMEM((STEPS, nz, nrec), bf16),
            pltpu.VMEM((nz, 2 * nz), bf16),
            pltpu.VMEM((nz, nz // 2), bf16),
            pltpu.VMEM((2, 2, 2, CHUNK * ny, LANES), f32),
            pltpu.VMEM((2, ny, LANES), f32),
            pltpu.VMEM((CHUNK // 2, 2, ny, LANES), f32),
            pltpu.VMEM((shots, ny // 2, nz // 2), f32),
            pltpu.VMEM((shots, ny // 2, nz // 2), f32),
            dma((12,)),
            dma((2,)),
            dma((2,)),
            dma((chunks, 2)),
            dma((chunks, 2)),
            dma((STEPS + 1, 2)),
            dma((STEPS + 1, 2)),
            dma((STEPS + 1, chunks, 2)),
            dma((STEPS + 1, chunks, 2)),
            dma((chunks, 2, 2)),
            dma((shots,)),
            dma((shots,)),
        ],
        compiler_params=pltpu.CompilerParams(
            collective_id=0, has_side_effects=True, vmem_limit_bytes=52 << 20
        ),
        name="window",
    )(
        stiffness, buoyancy, fwd_prev, fwd_now, adj_prev, adj_now, wavelet, source_cell,
        jnp.transpose(receiver_cell, (2, 0, 1)),
        jnp.transpose(traces, (0, 2, 1)),
        jnp.swapaxes(aperture_blocks, 3, 4),
        aperture_count,
    )


def solution(mesh):
    in_specs = (
        P("gx", "gy", None),
        P("gx", "gy", None),
        P("shot", "gx", "gy", None),
        P("shot", "gx", "gy", None),
        P("shot", "gx", "gy", None),
        P("shot", "gx", "gy", None),
        P("shot", None),
        P("shot", None),
        P("shot", None, None),
        P("shot", None, None),
        P(),
        P(),
    )
    out_specs = (
        P("shot", "gx", "gy", None),
        P("shot", "gx", "gy", None),
        P("gx", "shot", "gy", None),
    )
    return jax.shard_map(body, mesh=mesh, in_specs=in_specs, out_specs=out_specs, check_vma=False)
```

time: 490 us -> 57.2 us (0.12)
  the two profiles are of different devices: /device:TPU:1 before, /device:TPU:38 now
where the time goes in v1:
time: 57.2 us; the launch traced here: 56.9 us
  Pallas kernels  50.2 us (88%)
  local copies, waits for them, and re-layouts  6.08 us (11%)
  between operations  0.67 us (1%)
    pallas_call x1, Pallas kernels, body(): pl.pallas_call(kernel, out_shape=(jax.ShapeDtypeStruct(fwd_now.shape, f32...  50.2 us
    unnamed x15, local copies, waits for them, and re-layouts  6.08 us

profile of v1, /device:TPU:38, one launch (start us, length us, event | category | flops | bytes accessed | tf_op | source)
XLA Modules:
  0.0 56.9 jit_solution(1588760119895868599)
XLA Ops:
  0.6 0.0 copy-start.4
  0.6 0.0 copy-start.5
  0.7 0.6 %copy-done.4 = f32[1,4]{1,0:T(1,128)S(1)} copy-done((f32[1,4]{1,0:T(1,128)S(1)}, f32[1,4]{1,0:T(1,128)}, u32[]{:S(2)}) %copy-start.4) | copy-done | bytes 40
  1.3 0.0 copy-done.5
  1.3 0.0 copy-start
  1.3 0.8 %copy-done = s32[8,4,4,8,1]{3,4,2,1,0:T(1,128)S(1)} copy-done((s32[8,4,4,8,1]{3,4,2,1,0:T(1,128)S(1)}, s32[8,4,4,8,1]{3,4,2,1,0:T(1,128)}, u32[]{:S(2)}) %copy-start) | copy-done | bytes 4120
  2.1 0.0 copy-start.1
  2.1 0.8 %copy-done.1 = s32[8,4,4,8]{3,2,1,0:T(4,128)S(1)} copy-done((s32[8,4,4,8]{3,2,1,0:T(4,128)S(1)}, s32[8,4,4,8]{3,2,1,0:T(4,128)}, u32[]{:S(2)}) %copy-start.1) | copy-done | bytes 4120
  3.0 0.0 copy-start.2
  3.0 0.7 %copy-done.2 = f32[1,512,4]{1,2,0:T(4,128)S(1)} copy-done((f32[1,512,4]{1,2,0:T(4,128)S(1)}, f32[1,512,4]{1,2,0:T(4,128)}, u32[]{:S(2)}) %copy-start.2) | copy-done | bytes 8216
  3.7 0.0 copy-start.3
  3.7 0.7 %copy-done.3 = s32[1,512,3]{1,0,2:T(1,128)S(1)} copy-done((s32[1,512,3]{1,0,2:T(1,128)S(1)}, s32[1,512,3]{1,0,2:T(1,128)}, u32[]{:S(2)}) %copy-start.3) | copy-done | bytes 6168
  4.4 50.2 %window.1 = (f32[1,48,16,256]{3,2,1,0:T(8,128)S(1)}, f32[1,48,16,256]{3,2,1,0:T(8,128)S(1)}, f32[1,3,8,128]{3,2,1,0:T(8,128)S(1)}) custom-call(f32[48,16,256]{2,1,0:T(8,128)} %stiff.1, f32[48,16,256]{2,1,0:T(8,128)} %buoy.1, f32[1,48,16,256]{3,2,1,0:T(8,128)} %fwd0.1, f32[1,48,16,256]{3,2,1,0:T(8,128)} %fwd1.1, f32[1,48,16,256]{3,2,1,0:T(8,128)} %adj0.1, ...), custom_call_target="tpu_custom_call" | custom-call | tf_op jit(solution)/shard_map/window/pallas_call | solution.py:536
  54.6 0.9 %copy.18 = f32[1,48,16,256]{3,2,1,0:T(8,128)} copy(f32[1,48,16,256]{3,2,1,0:T(8,128)S(1)} %get-tuple-element.6) | data formatting | bytes 1572864
  55.5 0.9 %copy.19 = f32[1,48,16,256]{3,2,1,0:T(8,128)} copy(f32[1,48,16,256]{3,2,1,0:T(8,128)S(1)} %get-tuple-element.7) | data formatting | bytes 1572864
  56.3 0.6 %copy.20 = f32[1,3,8,128]{3,2,1,0:T(8,128)} copy(f32[1,3,8,128]{3,2,1,0:T(8,128)S(1)} %get-tuple-element.8) | data formatting | bytes 24576
Async XLA Ops:
  0.6 0.7 %copy-start.4 = (f32[1,4]{1,0:T(1,128)S(1)}, f32[1,4]{1,0:T(1,128)}, u32[]{:S(2)}) copy-start(f32[1,4]{1,0:T(1,128)} %wave.1) | copy-start | bytes 52
  0.6 0.7 %copy-start.5 = (s32[1,3]{1,0:T(1,128)S(1)}, s32[1,3]{1,0:T(1,128)}, u32[]{:S(2)}) copy-start(s32[1,3]{1,0:T(1,128)} %source.1) | copy-start | bytes 40
  1.3 0.8 %copy-start = (s32[8,4,4,8,1]{3,4,2,1,0:T(1,128)S(1)}, s32[8,4,4,8,1]{3,4,2,1,0:T(1,128)}, u32[]{:S(2)}) copy-start(s32[8,4,4,8,1]{3,4,2,1,0:T(1,128)} %param.22) | copy-start | bytes 12292
  2.1 0.8 %copy-start.1 = (s32[8,4,4,8]{3,2,1,0:T(4,128)S(1)}, s32[8,4,4,8]{3,2,1,0:T(4,128)}, u32[]{:S(2)}) copy-start(s32[8,4,4,8]{3,2,1,0:T(4,128)} %counts.1) | copy-start | bytes 12292
  3.0 0.7 %copy-start.2 = (f32[1,512,4]{1,2,0:T(4,128)S(1)}, f32[1,512,4]{1,2,0:T(4,128)}, u32[]{:S(2)}) copy-start(f32[1,512,4]{1,2,0:T(4,128)} %param.21) | copy-start | bytes 24580
  3.7 0.7 %copy-start.3 = (s32[1,512,3]{1,0,2:T(1,128)S(1)}, s32[1,512,3]{1,0,2:T(1,128)}, u32[]{:S(2)}) copy-start(s32[1,512,3]{1,0,2:T(1,128)} %param.20) | copy-start | bytes 18436

commit v2 on v1

v2 whole, which is shorter than its diff:
```python
import jax
import jax.numpy as jnp
from jax import lax
from jax.experimental import pallas as pl
from jax.experimental.pallas import tpu as pltpu
from jax.sharding import PartitionSpec as P

MESH = pl.DeviceIdType.MESH
STEPS = 4
WIDTH = 4
BLOCK = 24
CHUNK = 6
TOP = 8
LANES = 128

C1, D1 = 8.0 / 5.0, 4.0 / 5.0
second = tuple(c / C1 for c in (-205.0 / 72.0, 8.0 / 5.0, -1.0 / 5.0, 8.0 / 315.0, -1.0 / 560.0))
first = tuple(d / D1 for d in (4.0 / 5.0, -1.0 / 5.0, 4.0 / 105.0, -1.0 / 280.0))


def split(v):
    high = v.astype(jnp.bfloat16)
    return high, (v - high.astype(jnp.float32)).astype(jnp.bfloat16)


def dot(a, b):
    return jnp.dot(a, b, preferred_element_type=jnp.float32)


def dot_nt(a, b):
    return lax.dot_general(a, b, (((1,), (1,)), ((), ())), preferred_element_type=jnp.float32)


def kernel(
    stiff, buoy, fwd0, fwd1, adj0, adj1, wave_in, source_in, receiver_in, traces_in, blocks_in, counts_in,
    fwd_out, adj_out, grad_out,
    F0, F1, F2, F3, F4, F5, K, CO, R, Q, A, BH, BL, CZ, PZ, Z0, Z1, SM, TI, OUTG, INC,
    receiver, traces, wave, source, blocks, counts,
    load_sem, x_send, x_recv, y_send, y_recv, out_sem, g_send, g_recv,
):
    levels = (F0, F1, F2, F3, F4, F5)
    depth = (Z0, Z1)
    B = F1.at[2]
    nx, ny, nz = stiff.shape
    chunks = nx // CHUNK
    gx, gy, me = lax.axis_index("gx"), lax.axis_index("gy"), lax.axis_index("shot")
    last_x, last_y = lax.axis_size("gx") - 1, lax.axis_size("gy") - 1
    shots = lax.axis_size("shot")
    own = pl.ds(TOP, ny)
    inner = pl.ds(WIDTH, nx)
    sides_x = ((gx > 0, gx - 1), (gx < last_x, gx + 1))
    sides_y = ((gy > 0, gy - 1), (gy < last_y, gy + 1))

    def for_sides(sides, do):
        for side, (there, index) in enumerate(sides):
            @pl.when(there)
            def _():
                do(side, index)

    barrier = pltpu.get_barrier_semaphore()
    peers = shots - 1
    for axis, sides in (("gx", sides_x), ("gy", sides_y)):
        for there, index in sides:
            @pl.when(there)
            def _():
                pl.semaphore_signal(barrier, inc=1, device_id={axis: index}, device_id_type=MESH)
            peers = peers + jnp.where(there, 1, 0)

    def greet(step, _):
        pl.semaphore_signal(
            barrier, inc=1, device_id={"shot": lax.rem(me + step, shots)}, device_id_type=MESH
        )
        return 0

    lax.fori_loop(1, shots, greet, 0)

    small = [
        pltpu.make_async_copy(src, dst, load_sem.at[6 + i])
        for i, (src, dst) in enumerate(
            (
                (receiver_in, receiver),
                (traces_in, traces),
                (wave_in, wave),
                (source_in, source),
                (blocks_in.at[:, gx, gy], blocks),
                (counts_in.at[:, gx], counts),
            )
        )
    ]
    large = (
        (buoy, F1.at[2, inner, :, own, :]),
        (fwd1.at[0], F1.at[0, inner, :, own, :]),
        (adj1.at[0], F1.at[1, inner, :, own, :]),
        (stiff, K),
        (fwd0.at[0], F0.at[0, inner, :, own, :]),
        (adj0.at[0], F0.at[1, inner, :, own, :]),
    )

    def load(i):
        src, dst = large[i]
        for half in range(2):
            pltpu.make_async_copy(
                src.at[:, :, pl.ds(half * LANES, LANES)], dst.at[:, half], load_sem.at[i]
            ).start()

    def loaded(i):
        dst = large[i][1]
        pltpu.make_async_copy(dst, dst, load_sem.at[i]).wait()

    for copy in small[:4]:
        copy.start()
    for i in range(6):
        load(i)
    for copy in small[4:]:
        copy.start()

    for side, (there, _) in enumerate(sides_x):
        @pl.when(jnp.logical_not(there))
        def _():
            at = pl.ds(side * (nx + WIDTH), WIDTH)
            for ref in levels[1 : STEPS + 1]:
                for field in range(ref.shape[0]):
                    ref[field, at, :, own, :] = jnp.zeros((WIDTH, 2, ny, LANES), jnp.float32)
    for side, (there, _) in enumerate(sides_y):
        @pl.when(jnp.logical_not(there))
        def _():
            at = pl.ds(TOP - WIDTH + side * (ny + WIDTH), WIDTH)

            def clear(x, _):
                for ref in levels[1 : STEPS + 1]:
                    for field in range(ref.shape[0]):
                        ref[field, x, :, at, :] = jnp.zeros((2, WIDTH, LANES), jnp.float32)
                return 0

            lax.fori_loop(WIDTH, nx + WIDTH, clear, 0)

    def x_edge(side):
        return pl.ds(WIDTH + side * (nx - WIDTH), WIDTH), pl.ds((1 - side) * (nx + WIDTH), WIDTH)

    def y_edge(side):
        return (
            pl.ds(TOP + side * (ny - WIDTH), WIDTH),
            pl.ds(TOP - WIDTH + (1 - side) * (ny + WIDTH), WIDTH),
        )

    def x_copy(level, side, index, arrival=False):
        ref = levels[level]
        mine, theirs = x_edge(1 - side if arrival else side)
        return pltpu.make_async_remote_copy(
            src_ref=ref.at[:, theirs if arrival else mine, :, own, :],
            dst_ref=ref.at[:, theirs, :, own, :],
            send_sem=x_send.at[side],
            recv_sem=x_recv.at[level % 2, side if arrival else 1 - side],
            device_id={"gx": index},
            device_id_type=MESH,
        )

    def y_copy(level, chunk, side, index, arrival=False):
        ref = levels[level]
        mine, theirs = y_edge(1 - side if arrival else side)
        x = pl.ds(WIDTH + chunk * CHUNK, CHUNK)
        return pltpu.make_async_remote_copy(
            src_ref=ref.at[:, x, :, theirs if arrival else mine, :],
            dst_ref=ref.at[:, x, :, theirs, :],
            send_sem=y_send.at[chunk, side],
            recv_sem=y_recv.at[level % 2, chunk, side if arrival else 1 - side],
            device_id={"gy": index},
            device_id_type=MESH,
        )

    def order(i):
        return lax.rem(chunks - i, chunks)

    def on_border(chunk, do):
        for side, border in enumerate((0, chunks - 1)):
            there, index = sides_x[side]

            @pl.when((chunk == border) & there)
            def _():
                do(side, index)

    def await_halos(level, chunk):
        on_border(chunk, lambda side, index: x_copy(level, side, index, True).wait_recv())
        for_sides(sides_y, lambda side, index: y_copy(level, chunk, side, index, True).wait_recv())

    diff = lax.broadcasted_iota(jnp.int32, (nz, nz), 0) - lax.broadcasted_iota(jnp.int32, (nz, nz), 1)
    lap = jnp.zeros((nz, nz), jnp.float32)
    der = jnp.zeros((nz, nz), jnp.float32)
    for reach in range(1, WIDTH + 1):
        lap = jnp.where(jnp.abs(diff) == reach, second[reach], lap)
        der = jnp.where(diff == reach, first[reach - 1], der)
        der = jnp.where(diff == -reach, -first[reach - 1], der)
    CZ[:, 0:nz] = lap.astype(jnp.bfloat16)
    CZ[:, nz:] = der.astype(jnp.bfloat16)
    fine = lax.broadcasted_iota(jnp.int32, (nz, nz // 2), 0)
    pair = lax.broadcasted_iota(jnp.int32, (nz, nz // 2), 1) * 2
    PZ[...] = jnp.where((fine == pair) | (fine == pair + 1), 0.125, 0.0).astype(jnp.bfloat16)

    for copy in small[:4]:
        copy.wait()

    for half in range(2):
        row = lax.broadcasted_iota(jnp.int32, (ny, LANES), 0) + gy * ny
        col = lax.broadcasted_iota(jnp.int32, (ny, LANES), 1) + half * LANES
        SM[half] = jnp.where((row == source[0, 1]) & (col == source[0, 2]), 1.0, 0.0)

    rec_x = receiver[0] - gx * nx
    rec_y = receiver[1] - gy * ny
    inside = (rec_x >= 0) & (rec_x < nx) & (rec_y >= 0) & (rec_y < ny)
    cell = jnp.where(inside, rec_x * ny + rec_y, -1)
    nrec = cell.shape[1]
    rows = 128

    def hot(g, _):
        at = lax.broadcasted_iota(jnp.int32, (rows, nrec), 0) + g * rows
        A[pl.ds(pl.multiple_of(g * rows, rows), rows), :] = jnp.where(at == cell, 1.0, 0.0).astype(
            jnp.bfloat16
        )
        return 0

    lax.fori_loop(0, nx * ny // rows, hot, 0)
    rec_z = receiver[2]
    for n in range(STEPS):
        def place(g, _):
            at = lax.broadcasted_iota(jnp.int32, (64, nrec), 0) + g * 64
            high, low = split(jnp.where(at == rec_z, traces[0, n : n + 1, :], 0.0))
            where = pl.ds(pl.multiple_of(g * 64, 64), 64)
            BH[n, where, :] = high
            BL[n, where, :] = low
            return 0

        lax.fori_loop(0, nz // 64, place, 0)

    def inject(n, _):
        for part in range(2):
            hots = A[pl.ds(part * nx * ny // 2, nx * ny // 2), :]
            field = dot_nt(hots, BH[n]) + dot_nt(hots, BL[n])
            field = field.reshape(nx // 2, ny, nz)
            for half in range(2):
                R[n, pl.ds(part * nx // 2, nx // 2), half] = field[:, :, half * LANES : (half + 1) * LANES]
        return 0

    lax.fori_loop(0, STEPS, inject, 0)

    for i in range(3):
        loaded(i)
    pl.semaphore_wait(barrier, peers)
    for_sides(sides_x, lambda side, index: x_copy(1, side, index).start())

    def first_strips(i, _):
        for_sides(sides_y, lambda side, index: y_copy(1, order(i), side, index).start())
        return 0

    lax.fori_loop(0, chunks, first_strips, 0)

    def along_depth(ref, block, out_ref):
        x = pl.ds(WIDTH + block * BLOCK, BLOCK)
        cells = BLOCK * ny
        parts = [
            jnp.concatenate(
                [ref[field, x, half, own, :].reshape(cells, LANES) for half in range(2)], axis=1
            )
            for field in range(2)
        ]
        high, low = split(jnp.concatenate(parts, axis=0))
        out = dot(high, CZ[...]) + dot(low, CZ[...])
        for field in range(2):
            for kind in range(2):
                for half in range(2):
                    at = kind * nz + half * LANES
                    piece = out[field * cells : (field + 1) * cells, at : at + LANES]
                    out_ref[field, kind, pl.ds(block * BLOCK, BLOCK), half] = piece.reshape(
                        BLOCK, ny, LANES
                    )

    def slopes(along, x, half):
        total = None
        for reach in range(1, WIDTH + 1):
            if along == 0:
                ahead, behind = B[x + reach, half, own, :], B[x - reach, half, own, :]
            else:
                ahead = B[x, half, pl.ds(TOP + reach, ny), :]
                behind = B[x, half, pl.ds(TOP - reach, ny), :]
            term = ahead - behind
            if reach > 1:
                term = first[reach - 1] * term
            total = term if total is None else total + term
        return total

    loaded(3)

    def prepare(chunk, _):
        x = pl.ds(WIDTH + chunk * CHUNK, CHUNK)
        xk = pl.ds(chunk * CHUNK, CHUNK)
        parts = [B[x, half, own, :].reshape(CHUNK * ny, LANES) for half in range(2)]
        high, low = split(jnp.concatenate(parts, axis=1))
        der_z = dot(high, CZ[:, nz:]) + dot(low, CZ[:, nz:])
        for half in range(2):
            stiffness = K[xk, half]
            CO[0, xk, half] = C1 * stiffness * parts[half].reshape(CHUNK, ny, LANES)
            along = der_z[:, half * LANES : (half + 1) * LANES].reshape(CHUNK, ny, LANES)
            CO[3, xk, half] = (D1 * D1) * stiffness * along
        return 0

    lax.fori_loop(0, chunks, prepare, 0)

    def all_depths(level):
        def one(block, _):
            along_depth(levels[level], block, depth[(level + 1) % 2])
            return 0

        lax.fori_loop(0, nx // BLOCK, one, 0)

    all_depths(1)

    def coefficients(chunk):
        def plane(j, _):
            x = chunk * CHUNK + j
            for half in range(2):
                stiffness = (D1 * D1) * K[x, half]
                CO[1, x, half] = stiffness * slopes(0, WIDTH + x, half)
                CO[2, x, half] = stiffness * slopes(1, WIDTH + x, half)
            return 0

        lax.fori_loop(0, CHUNK, plane, 0)

    for i in (4, 5):
        loaded(i)

    def stencil(n, chunk, half):
        before, now, after = levels[n], levels[n + 1], levels[n + 2]
        x0 = chunk * CHUNK
        amplitudes = [
            jnp.where(source[0, 0] - gx * nx == x0 + j, wave[0, n], 0.0) for j in range(CHUNK)
        ]
        for top in range(0, ny, 8):
            tile = pl.ds(TOP + top, 8)
            row = pl.ds(top, 8)
            planes = [
                [now[field, x0 + k, half, tile, :] for k in range(CHUNK + 2 * WIDTH)]
                for field in range(2)
            ]
            for j in range(CHUNK):
                x = x0 + j
                co = [CO[i, x, half, row, :] for i in range(4)]
                for field in range(2):
                    xs = planes[field]
                    here = xs[WIDTH + j]
                    lap = (3.0 * second[0]) * here + depth[n % 2][field, 0, x, half, row, :]
                    der_x = der_y = None
                    for reach in range(1, WIDTH + 1):
                        xa, xb = xs[WIDTH + j + reach], xs[WIDTH + j - reach]
                        ya = now[field, x + WIDTH, half, pl.ds(TOP + top + reach, 8), :]
                        yb = now[field, x + WIDTH, half, pl.ds(TOP + top - reach, 8), :]
                        pairs = (xa + xb) + (ya + yb)
                        dx, dy = xa - xb, ya - yb
                        if reach == 1:
                            lap, der_x, der_y = lap + pairs, dx, dy
                        else:
                            lap = lap + second[reach] * pairs
                            der_x = der_x + first[reach - 1] * dx
                            der_y = der_y + first[reach - 1] * dy
                    change = co[0] * lap + co[1] * der_x + co[2] * der_y
                    change = change + co[3] * depth[n % 2][field, 1, x, half, row, :]
                    if field == 0:
                        change = change + amplitudes[j] * SM[half, row, :]
                        Q[n, x, half, row, :] = change
                    else:
                        change = change + R[n, x, half, row, :]
                    old = before[field, x + WIDTH, half, tile, :]
                    after[field, x + WIDTH, half, tile, :] = (2.0 * here - old) + change

    def send_on(level, chunk):
        def face(side, index):
            x_copy(level - 1, side, index).wait_send()
            x_copy(level, side, index).start()

        def strip(side, index):
            y_copy(level - 1, chunk, side, index).wait_send()
            y_copy(level, chunk, side, index).start()

        on_border(chunk, face)
        for_sides(sides_y, strip)

    def out_copies(x):
        for field, out in enumerate((fwd_out, adj_out)):
            for half in range(2):
                yield pltpu.make_async_copy(
                    F5.at[field, pl.ds(WIDTH + x.start, x.size), half, own, :],
                    out.at[0, x, :, pl.ds(half * LANES, LANES)],
                    out_sem.at[field, half],
                )

    def chosen(shot, owner, k):
        valid = (blocks[shot, 0, owner] == k) & (counts[shot, gy, owner] > 0)
        return jnp.where(valid, 1.0, 0.0)

    def imaging(chunk):
        for copy in out_copies(pl.ds(chunk * CHUNK, CHUNK)):
            copy.start()
        x0 = chunk * CHUNK
        for k in range(CHUNK // 2):
            for half in range(2):
                total = None
                for odd in range(2):
                    x = x0 + 2 * k + odd
                    for later in range(2, STEPS + 2):
                        term = levels[later][1, x + WIDTH, half, own, :] * Q[STEPS + 1 - later, x, half]
                        total = term if total is None else total + term
                TI[k, half] = total
        rows_k = []
        for k in range(CHUNK // 2):
            halves = [
                TI[k, half, pl.ds(0, ny // 2, stride=2), :] + TI[k, half, pl.ds(1, ny // 2, stride=2), :]
                for half in range(2)
            ]
            rows_k.append(jnp.concatenate(halves, axis=1))
        high, low = split(jnp.concatenate(rows_k, axis=0))
        coarse = dot(high, PZ[...]) + dot(low, PZ[...])
        row = None
        for k in range(CHUNK // 2):
            term = chosen(me, chunk, k) * coarse[k * (ny // 2) : (k + 1) * (ny // 2), :]
            row = term if row is None else row + term

        @pl.when(chunk == me)
        def _():
            INC[me] = row

        @pl.when(chunk != me)
        def _():
            OUTG[chunk] = row
            pltpu.make_async_remote_copy(
                src_ref=OUTG.at[chunk],
                dst_ref=INC.at[me],
                send_sem=g_send,
                recv_sem=g_recv,
                device_id={"shot": chunk},
                device_id_type=MESH,
            ).start()

    for copy in small[4:]:
        copy.wait()

    for n in range(STEPS):
        def run(i, _):
            chunk = order(i)
            await_halos(n + 1, chunk)
            if n == 0:
                coefficients(chunk)
            def part(half, _):
                stencil(n, chunk, half)
                return 0

            lax.fori_loop(0, 2, part, 0)
            if n < STEPS - 1:
                send_on(n + 2, chunk)
            else:
                imaging(chunk)
            return 0

        lax.fori_loop(0, chunks, run, 0)
        if n < STEPS - 1:
            all_depths(n + 2)

    others = pltpu.make_async_remote_copy(
        src_ref=OUTG.at[pl.ds(0, shots - 1)],
        dst_ref=INC.at[pl.ds(0, shots - 1)],
        send_sem=g_send,
        recv_sem=g_recv,
        device_id={"shot": lax.rem(me + 1, shots)},
        device_id_type=MESH,
    )
    others.wait_recv()
    for k in range(CHUNK // 2):
        total = None
        for shot in range(shots):
            term = chosen(shot, me, k) * INC[shot]
            total = term if total is None else total + term
        grad_out[0, k] = total

    others.wait_send()
    for copy in out_copies(pl.ds(0, nx)):
        copy.wait()

    def done(chunk, _):
        for_sides(sides_y, lambda side, index: y_copy(STEPS, chunk, side, index).wait_send())
        return 0

    lax.fori_loop(0, chunks, done, 0)
    for_sides(sides_x, lambda side, index: x_copy(STEPS, side, index).wait_send())


def hand_on(fwd, adj, grad, fwd_out, adj_out, grad_out, fwd_here, adj_here, grad_here, sems):
    pieces = 4
    size = fwd.shape[1] // pieces
    ways = [(grad, grad_here, grad_out)]
    for src, here, dst in ((fwd, fwd_here, fwd_out), (adj, adj_here, adj_out)):
        for p in range(pieces):
            x = pl.ds(p * size, size)
            ways.append((src.at[:, x], here.at[:, x], dst.at[:, x]))
    ways = [
        (pltpu.make_async_copy(src, here, sems.at[0, i]), pltpu.make_async_copy(here, dst, sems.at[1, i]))
        for i, (src, here, dst) in enumerate(ways)
    ]
    for arrive, _ in ways:
        arrive.start()
    for arrive, leave in ways:
        arrive.wait()
        leave.start()
    for _, leave in ways:
        leave.wait()


def body(
    stiffness, buoyancy, fwd_prev, fwd_now, adj_prev, adj_now, wavelet, source_cell, receiver_cell,
    traces, aperture_blocks, aperture_count,
):
    nx, ny, nz = stiffness.shape
    shots = lax.axis_size("shot")
    nrec = traces.shape[1]
    chunks = nx // CHUNK
    xe, ye = nx + 2 * WIDTH, ny + 2 * TOP
    f32, bf16, i32 = jnp.float32, jnp.bfloat16, jnp.int32
    hbm = pl.BlockSpec(memory_space=pltpu.HBM)
    vmem = pl.BlockSpec(memory_space=pltpu.VMEM)
    dma = pltpu.SemaphoreType.DMA
    receivers = jnp.transpose(receiver_cell, (2, 0, 1))
    by_step = jnp.transpose(traces, (0, 2, 1))
    lists = jnp.swapaxes(aperture_blocks, 3, 4)
    out_shape = (
        jax.ShapeDtypeStruct(fwd_now.shape, f32),
        jax.ShapeDtypeStruct(adj_now.shape, f32),
        jax.ShapeDtypeStruct((1, nx // 2 // shots, ny // 2, nz // 2), f32),
    )
    results = pl.pallas_call(
        kernel,
        out_shape=out_shape,
        in_specs=[hbm] * 12,
        out_specs=(pl.BlockSpec(memory_space=pl.ANY),) * 2 + (vmem,),
        scratch_shapes=[
            pltpu.VMEM((2, xe, 2, ye, LANES), f32),
            pltpu.VMEM((3, xe, 2, ye, LANES), f32),
            pltpu.VMEM((2, xe, 2, ye, LANES), f32),
            pltpu.VMEM((2, xe, 2, ye, LANES), f32),
            pltpu.VMEM((2, xe, 2, ye, LANES), f32),
            pltpu.VMEM((2, xe, 2, ye, LANES), f32),
            pltpu.VMEM((nx, 2, ny, LANES), f32),
            pltpu.VMEM((4, nx, 2, ny, LANES), f32),
            pltpu.VMEM((STEPS, nx, 2, ny, LANES), f32),
            pltpu.VMEM((STEPS, nx, 2, ny, LANES), f32),
            pltpu.VMEM((nx * ny, nrec), bf16),
            pltpu.VMEM((STEPS, nz, nrec), bf16),
            pltpu.VMEM((STEPS, nz, nrec), bf16),
            pltpu.VMEM((nz, 2 * nz), bf16),
            pltpu.VMEM((nz, nz // 2), bf16),
            pltpu.VMEM((2, 2, nx, 2, ny, LANES), f32),
            pltpu.VMEM((2, 2, nx, 2, ny, LANES), f32),
            pltpu.VMEM((2, ny, LANES), f32),
            pltpu.VMEM((CHUNK // 2, 2, ny, LANES), f32),
            pltpu.VMEM((shots, ny // 2, nz // 2), f32),
            pltpu.VMEM((shots, ny // 2, nz // 2), f32),
            pltpu.VMEM(receivers.shape, i32),
            pltpu.VMEM(by_step.shape, f32),
            pltpu.SMEM(wavelet.shape, f32),
            pltpu.SMEM(source_cell.shape, i32),
            pltpu.SMEM((shots,) + lists.shape[3:], i32),
            pltpu.SMEM((shots,) + aperture_count.shape[2:], i32),
            dma((12,)),
            dma((2,)),
            dma((2, 2)),
            dma((chunks, 2)),
            dma((2, chunks, 2)),
            dma((2, 2)),
            dma(()),
            dma(()),
        ],
        compiler_params=pltpu.CompilerParams(
            collective_id=0, has_side_effects=True, vmem_limit_bytes=60 << 20
        ),
        name="window",
    )(
        stiffness, buoyancy, fwd_prev, fwd_now, adj_prev, adj_now, wavelet, source_cell,
        receivers, by_step, lists, aperture_count,
    )
    return pl.pallas_call(
        hand_on,
        out_shape=out_shape,
        in_specs=[hbm] * 3,
        out_specs=(hbm,) * 3,
        scratch_shapes=[pltpu.VMEM(out.shape, f32) for out in out_shape] + [dma((2, 9))],
        name="hand_on",
    )(*results)


def solution(mesh):
    in_specs = (
        P("gx", "gy", None),
        P("gx", "gy", None),
        P("shot", "gx", "gy", None),
        P("shot", "gx", "gy", None),
        P("shot", "gx", "gy", None),
        P("shot", "gx", "gy", None),
        P("shot", None),
        P("shot", None),
        P("shot", None, None),
        P("shot", None, None),
        P(),
        P(),
    )
    out_specs = (
        P("shot", "gx", "gy", None),
        P("shot", "gx", "gy", None),
        P("gx", "shot", "gy", None),
    )
    return jax.shard_map(body, mesh=mesh, in_specs=in_specs, out_specs=out_specs, check_vma=False)
```

time: 57.2 us -> 40.6 us (0.71)
  Pallas kernels: 50.2 us -> 39.8 us
  local copies, waits for them, and re-layouts: 6.08 us -> 0 us
    pallas_call x1 -> x2, Pallas kernels: 50.2 us -> 39.8 us  [the longest x1 37.5 us: body(): pl.pallas_call(kernel, out_shape=out_shape, in_specs=[hbm] * 12, out_spec...]
    unnamed x15 -> x0, local copies, waits for them, and re-layouts: 6.08 us -> none
where the time goes in v2:
time: 40.6 us; the launch traced here: 40.4 us
  Pallas kernels  39.8 us (98%)
  between operations  0.64 us (2%)
    pallas_call x1, Pallas kernels, body(): pl.pallas_call(kernel, out_shape=out_shape, in_specs=[hbm] * 12, out_spec...  37.5 us
    pallas_call x1, Pallas kernels, body(): pl.pallas_call(hand_on, out_shape=out_shape, in_specs=[hbm] * 3, out_spec...  2.32 us

profile of v2, /device:TPU:38, one launch (start us, length us, event | category | flops | bytes accessed | tf_op | source)
XLA Modules:
  0.0 40.4 jit_solution(13462305432710365663)
XLA Ops:
  0.6 37.5 %window.1 = (f32[1,48,16,256]{3,2,1,0:T(8,128)}, f32[1,48,16,256]{3,2,1,0:T(8,128)}, f32[1,3,8,128]{3,2,1,0:T(8,128)}) custom-call(f32[48,16,256]{2,1,0:T(8,128)} %stiff.1, f32[48,16,256]{2,1,0:T(8,128)} %buoy.1, f32[1,48,16,256]{3,2,1,0:T(8,128)} %fwd0.1, f32[1,48,16,256]{3,2,1,0:T(8,128)} %fwd1.1, f32[1,48,16,256]{3,2,1,0:T(8,128)} %adj0.1, ...), custom_call_target="tpu_custom_call" | custom-call | tf_op jit(solution)/shard_map/window/pallas_call | solution.py:535
  38.1 2.3 %hand_on.1 = (f32[1,48,16,256]{3,2,1,0:T(8,128)}, f32[1,48,16,256]{3,2,1,0:T(8,128)}, f32[1,3,8,128]{3,2,1,0:T(8,128)}) custom-call(f32[1,48,16,256]{3,2,1,0:T(8,128)} %get-tuple-element.6.fwd, f32[1,48,16,256]{3,2,1,0:T(8,128)} %get-tuple-element.7.adj, f32[1,3,8,128]{3,2,1,0:T(8,128)} %get-tuple-element.8.grad), custom_call_target="tpu_custom_call" | custom-call | tf_op jit(solution)/shard_map/hand_on/pallas_call | solution.py:585

commit v3 on v2

--- a/solution.py
+++ b/solution.py
@@ -183,6 +183,17 @@
         on_border(chunk, lambda side, index: x_copy(level, side, index, True).wait_recv())
         for_sides(sides_y, lambda side, index: y_copy(level, chunk, side, index, True).wait_recv())
 
+    for i in range(3):
+        loaded(i)
+    pl.semaphore_wait(barrier, peers)
+    for_sides(sides_x, lambda side, index: x_copy(1, side, index).start())
+
+    def first_strips(i, _):
+        for_sides(sides_y, lambda side, index: y_copy(1, order(i), side, index).start())
+        return 0
+
+    lax.fori_loop(0, chunks, first_strips, 0)
+
     diff = lax.broadcasted_iota(jnp.int32, (nz, nz), 0) - lax.broadcasted_iota(jnp.int32, (nz, nz), 1)
     lap = jnp.zeros((nz, nz), jnp.float32)
     der = jnp.zeros((nz, nz), jnp.float32)
@@ -241,17 +252,6 @@
         return 0
 
     lax.fori_loop(0, STEPS, inject, 0)
-
-    for i in range(3):
-        loaded(i)
-    pl.semaphore_wait(barrier, peers)
-    for_sides(sides_x, lambda side, index: x_copy(1, side, index).start())
-
-    def first_strips(i, _):
-        for_sides(sides_y, lambda side, index: y_copy(1, order(i), side, index).start())
-        return 0
-
-    lax.fori_loop(0, chunks, first_strips, 0)
 
     def along_depth(ref, block, out_ref):
         x = pl.ds(WIDTH + block * BLOCK, BLOCK)
@@ -289,20 +289,20 @@
 
     loaded(3)
 
-    def prepare(chunk, _):
-        x = pl.ds(WIDTH + chunk * CHUNK, CHUNK)
-        xk = pl.ds(chunk * CHUNK, CHUNK)
-        parts = [B[x, half, own, :].reshape(CHUNK * ny, LANES) for half in range(2)]
+    def prepare(block, _):
+        x = pl.ds(WIDTH + block * BLOCK, BLOCK)
+        xk = pl.ds(block * BLOCK, BLOCK)
+        parts = [B[x, half, own, :].reshape(BLOCK * ny, LANES) for half in range(2)]
         high, low = split(jnp.concatenate(parts, axis=1))
         der_z = dot(high, CZ[:, nz:]) + dot(low, CZ[:, nz:])
         for half in range(2):
             stiffness = K[xk, half]
-            CO[0, xk, half] = C1 * stiffness * parts[half].reshape(CHUNK, ny, LANES)
-            along = der_z[:, half * LANES : (half + 1) * LANES].reshape(CHUNK, ny, LANES)
+            CO[0, xk, half] = C1 * stiffness * parts[half].reshape(BLOCK, ny, LANES)
+            along = der_z[:, half * LANES : (half + 1) * LANES].reshape(BLOCK, ny, LANES)
             CO[3, xk, half] = (D1 * D1) * stiffness * along
         return 0
 
-    lax.fori_loop(0, chunks, prepare, 0)
+    lax.fori_loop(0, nx // BLOCK, prepare, 0)
 
     def all_depths(level):
         def one(block, _):
@@ -382,12 +382,12 @@
         on_border(chunk, face)
         for_sides(sides_y, strip)
 
-    def out_copies(x):
+    def out_copies():
         for field, out in enumerate((fwd_out, adj_out)):
             for half in range(2):
                 yield pltpu.make_async_copy(
-                    F5.at[field, pl.ds(WIDTH + x.start, x.size), half, own, :],
-                    out.at[0, x, :, pl.ds(half * LANES, LANES)],
+                    F5.at[field, inner, half, own, :],
+                    out.at[0, :, :, pl.ds(half * LANES, LANES)],
                     out_sem.at[field, half],
                 )
 
@@ -396,8 +396,6 @@
         return jnp.where(valid, 1.0, 0.0)
 
     def imaging(chunk):
-        for copy in out_copies(pl.ds(chunk * CHUNK, CHUNK)):
-            copy.start()
         x0 = chunk * CHUNK
         for k in range(CHUNK // 2):
             for half in range(2):
@@ -447,11 +445,8 @@
             await_halos(n + 1, chunk)
             if n == 0:
                 coefficients(chunk)
-            def part(half, _):
+            for half in range(2):
                 stencil(n, chunk, half)
-                return 0
-
-            lax.fori_loop(0, 2, part, 0)
             if n < STEPS - 1:
                 send_on(n + 2, chunk)
             else:
@@ -461,6 +456,17 @@
         lax.fori_loop(0, chunks, run, 0)
         if n < STEPS - 1:
             all_depths(n + 2)
+
+    for copy in out_copies():
+        copy.start()
+    weights = [[chosen(shot, me, k) for shot in range(shots)] for k in range(CHUNK // 2)]
+
+    def done(chunk, _):
+        for_sides(sides_y, lambda side, index: y_copy(STEPS, chunk, side, index).wait_send())
+        return 0
+
+    lax.fori_loop(0, chunks, done, 0)
+    for_sides(sides_x, lambda side, index: x_copy(STEPS, side, index).wait_send())
 
     others = pltpu.make_async_remote_copy(
         src_ref=OUTG.at[pl.ds(0, shots - 1)],
@@ -470,24 +476,16 @@
         device_id={"shot": lax.rem(me + 1, shots)},
         device_id_type=MESH,
     )
+    others.wait_send()
+    for copy in out_copies():
+        copy.wait()
     others.wait_recv()
     for k in range(CHUNK // 2):
         total = None
         for shot in range(shots):
-            term = chosen(shot, me, k) * INC[shot]
+            term = weights[k][shot] * INC[shot]
             total = term if total is None else total + term
         grad_out[0, k] = total
-
-    others.wait_send()
-    for copy in out_copies(pl.ds(0, nx)):
-        copy.wait()
-
-    def done(chunk, _):
-        for_sides(sides_y, lambda side, index: y_copy(STEPS, chunk, side, index).wait_send())
-        return 0
-
-    lax.fori_loop(0, chunks, done, 0)
-    for_sides(sides_x, lambda side, index: x_copy(STEPS, side, index).wait_send())
 
 
 def hand_on(fwd, adj, grad, fwd_out, adj_out, grad_out, fwd_here, adj_here, grad_here, sems):

time: 40.6 us -> 38 us (0.936)
  Pallas kernels: 39.8 us -> 37.1 us
    pallas_call x1, Pallas kernels: 37.5 us -> 34.8 us  [body(): pl.pallas_call(kernel, out_shape=out_shape, in_specs=[hbm] * 12, out_spec...]
where the time goes in v3:
time: 38 us; the launch traced here: 37.8 us
  Pallas kernels  37.1 us (98%)
  between operations  0.64 us (2%)
    pallas_call x1, Pallas kernels, body(): pl.pallas_call(kernel, out_shape=out_shape, in_specs=[hbm] * 12, out_spec...  34.8 us
    pallas_call x1, Pallas kernels, body(): pl.pallas_call(hand_on, out_shape=out_shape, in_specs=[hbm] * 3, out_spec...  2.32 us

profile of v3, /device:TPU:38, one launch (start us, length us, event | category | flops | bytes accessed | tf_op | source)
XLA Modules:
  0.0 37.8 jit_solution(2805374715257967842)
XLA Ops:
  0.6 34.8 %window.1 = (f32[1,48,16,256]{3,2,1,0:T(8,128)}, f32[1,48,16,256]{3,2,1,0:T(8,128)}, f32[1,3,8,128]{3,2,1,0:T(8,128)}) custom-call(f32[48,16,256]{2,1,0:T(8,128)} %stiff.1, f32[48,16,256]{2,1,0:T(8,128)} %buoy.1, f32[1,48,16,256]{3,2,1,0:T(8,128)} %fwd0.1, f32[1,48,16,256]{3,2,1,0:T(8,128)} %fwd1.1, f32[1,48,16,256]{3,2,1,0:T(8,128)} %adj0.1, ...), custom_call_target="tpu_custom_call" | custom-call | tf_op jit(solution)/shard_map/window/pallas_call | solution.py:533
  35.5 2.3 %hand_on.1 = (f32[1,48,16,256]{3,2,1,0:T(8,128)}, f32[1,48,16,256]{3,2,1,0:T(8,128)}, f32[1,3,8,128]{3,2,1,0:T(8,128)}) custom-call(f32[1,48,16,256]{3,2,1,0:T(8,128)} %get-tuple-element.6.fwd, f32[1,48,16,256]{3,2,1,0:T(8,128)} %get-tuple-element.7.adj, f32[1,3,8,128]{3,2,1,0:T(8,128)} %get-tuple-element.8.grad), custom_call_target="tpu_custom_call" | custom-call | tf_op jit(solution)/shard_map/hand_on/pallas_call | solution.py:583

commit v4 on v3

--- a/solution.py
+++ b/solution.py
@@ -8,7 +8,7 @@
 MESH = pl.DeviceIdType.MESH
 STEPS = 4
 WIDTH = 4
-BLOCK = 24
+BLOCK = 48
 CHUNK = 6
 TOP = 8
 LANES = 128
@@ -419,7 +419,9 @@
         for k in range(CHUNK // 2):
             term = chosen(me, chunk, k) * coarse[k * (ny // 2) : (k + 1) * (ny // 2), :]
             row = term if row is None else row + term
-
+        return row
+
+    def deliver(chunk, row):
         @pl.when(chunk == me)
         def _():
             INC[me] = row
@@ -445,17 +447,24 @@
             await_halos(n + 1, chunk)
             if n == 0:
                 coefficients(chunk)
+            if n == STEPS - 1:
+                earlier = order(lax.rem(i + chunks - 1, chunks))
+                row = imaging(earlier)
             for half in range(2):
                 stencil(n, chunk, half)
             if n < STEPS - 1:
                 send_on(n + 2, chunk)
             else:
-                imaging(chunk)
+                @pl.when(i > 0)
+                def _():
+                    deliver(earlier, row)
             return 0
 
         lax.fori_loop(0, chunks, run, 0)
         if n < STEPS - 1:
             all_depths(n + 2)
+        else:
+            deliver(order(chunks - 1), imaging(order(chunks - 1)))
 
     for copy in out_copies():
         copy.start()

time: 38 us -> 37.5 us (0.987)
  Pallas kernels: 37.1 us -> 36.7 us
    pallas_call x1, Pallas kernels: 34.8 us -> 34.4 us  [body(): pl.pallas_call(kernel, out_shape=out_shape, in_specs=[hbm] * 12, out_spec...]
where the time goes in v4:
time: 37.5 us; the launch traced here: 37.4 us
  Pallas kernels  36.7 us (98%)
  between operations  0.64 us (2%)
    pallas_call x1, Pallas kernels, body(): pl.pallas_call(kernel, out_shape=out_shape, in_specs=[hbm] * 12, out_spec...  34.4 us
    pallas_call x1, Pallas kernels, body(): pl.pallas_call(hand_on, out_shape=out_shape, in_specs=[hbm] * 3, out_spec...  2.32 us

profile of v4, /device:TPU:38, one launch (start us, length us, event | category | flops | bytes accessed | tf_op | source)
XLA Modules:
  0.0 37.4 jit_solution(4549903212349243241)
XLA Ops:
  0.6 34.4 %window.1 = (f32[1,48,16,256]{3,2,1,0:T(8,128)}, f32[1,48,16,256]{3,2,1,0:T(8,128)}, f32[1,3,8,128]{3,2,1,0:T(8,128)}) custom-call(f32[48,16,256]{2,1,0:T(8,128)} %stiff.1, f32[48,16,256]{2,1,0:T(8,128)} %buoy.1, f32[1,48,16,256]{3,2,1,0:T(8,128)} %fwd0.1, f32[1,48,16,256]{3,2,1,0:T(8,128)} %fwd1.1, f32[1,48,16,256]{3,2,1,0:T(8,128)} %adj0.1, ...), custom_call_target="tpu_custom_call" | custom-call | tf_op jit(solution)/shard_map/window/pallas_call | solution.py:542
  35.0 2.3 %hand_on.1 = (f32[1,48,16,256]{3,2,1,0:T(8,128)}, f32[1,48,16,256]{3,2,1,0:T(8,128)}, f32[1,3,8,128]{3,2,1,0:T(8,128)}) custom-call(f32[1,48,16,256]{3,2,1,0:T(8,128)} %get-tuple-element.6.fwd, f32[1,48,16,256]{3,2,1,0:T(8,128)} %get-tuple-element.7.adj, f32[1,3,8,128]{3,2,1,0:T(8,128)} %get-tuple-element.8.grad), custom_call_target="tpu_custom_call" | custom-call | tf_op jit(solution)/shard_map/hand_on/pallas_call | solution.py:592

commit v5 on v4

--- a/solution.py
+++ b/solution.py
@@ -299,6 +299,7 @@
             stiffness = K[xk, half]
             CO[0, xk, half] = C1 * stiffness * parts[half].reshape(BLOCK, ny, LANES)
             along = der_z[:, half * LANES : (half + 1) * LANES].reshape(BLOCK, ny, LANES)
+            CO[4, xk, half] = 2.0 + (3.0 * second[0]) * CO[0, xk, half]
             CO[3, xk, half] = (D1 * D1) * stiffness * along
         return 0
 
@@ -346,7 +347,9 @@
                 for field in range(2):
                     xs = planes[field]
                     here = xs[WIDTH + j]
-                    lap = (3.0 * second[0]) * here + depth[n % 2][field, 0, x, half, row, :]
+                    lap = depth[n % 2][field, 0, x, half, row, :]
+                    if field == 0:
+                        lap = (3.0 * second[0]) * here + lap
                     der_x = der_y = None
                     for reach in range(1, WIDTH + 1):
                         xa, xb = xs[WIDTH + j + reach], xs[WIDTH + j - reach]
@@ -368,7 +371,9 @@
                     else:
                         change = change + R[n, x, half, row, :]
                     old = before[field, x + WIDTH, half, tile, :]
-                    after[field, x + WIDTH, half, tile, :] = (2.0 * here - old) + change
+                    after[field, x + WIDTH, half, tile, :] = (
+                        (2.0 if field == 0 else CO[4, x, half, row, :]) * here - old
+                    ) + change
 
     def send_on(level, chunk):
         def face(side, index):
@@ -552,7 +557,7 @@
             pltpu.VMEM((2, xe, 2, ye, LANES), f32),
             pltpu.VMEM((2, xe, 2, ye, LANES), f32),
             pltpu.VMEM((nx, 2, ny, LANES), f32),
-            pltpu.VMEM((4, nx, 2, ny, LANES), f32),
+            pltpu.VMEM((5, nx, 2, ny, LANES), f32),
             pltpu.VMEM((STEPS, nx, 2, ny, LANES), f32),
             pltpu.VMEM((STEPS, nx, 2, ny, LANES), f32),
             pltpu.VMEM((nx * ny, nrec), bf16),

time: 37.5 us -> 37.4 us (level)
  no operation moved by 1% of the time
where the time goes in v5:
time: 37.4 us; the launch traced here: 37.2 us
  Pallas kernels  36.6 us (98%)
  between operations  0.64 us (2%)
    pallas_call x1, Pallas kernels, body(): pl.pallas_call(kernel, out_shape=out_shape, in_specs=[hbm] * 12, out_spec...  34.3 us
    pallas_call x1, Pallas kernels, body(): pl.pallas_call(hand_on, out_shape=out_shape, in_specs=[hbm] * 3, out_spec...  2.32 us

profile of v5, /device:TPU:38, one launch (start us, length us, event | category | flops | bytes accessed | tf_op | source)
XLA Modules:
  0.0 37.2 jit_solution(7502182011594287117)
XLA Ops:
  0.6 34.3 %window.1 = (f32[1,48,16,256]{3,2,1,0:T(8,128)}, f32[1,48,16,256]{3,2,1,0:T(8,128)}, f32[1,3,8,128]{3,2,1,0:T(8,128)}) custom-call(f32[48,16,256]{2,1,0:T(8,128)} %stiff.1, f32[48,16,256]{2,1,0:T(8,128)} %buoy.1, f32[1,48,16,256]{3,2,1,0:T(8,128)} %fwd0.1, f32[1,48,16,256]{3,2,1,0:T(8,128)} %fwd1.1, f32[1,48,16,256]{3,2,1,0:T(8,128)} %adj0.1, ...), custom_call_target="tpu_custom_call" | custom-call | tf_op jit(solution)/shard_map/window/pallas_call | solution.py:547
  34.9 2.3 %hand_on.1 = (f32[1,48,16,256]{3,2,1,0:T(8,128)}, f32[1,48,16,256]{3,2,1,0:T(8,128)}, f32[1,3,8,128]{3,2,1,0:T(8,128)}) custom-call(f32[1,48,16,256]{3,2,1,0:T(8,128)} %get-tuple-element.6.fwd, f32[1,48,16,256]{3,2,1,0:T(8,128)} %get-tuple-element.7.adj, f32[1,3,8,128]{3,2,1,0:T(8,128)} %get-tuple-element.8.grad), custom_call_target="tpu_custom_call" | custom-call | tf_op jit(solution)/shard_map/hand_on/pallas_call | solution.py:597
